TPU v7x, 256 devices: a whole 4x4x8 slice. The times are simulated.
256 devices in a mesh: stn: 16 (over y, x_hi, core), tm: 16 (over z, x_lo).
Axes of the slice: x: 4 (x_hi: 2, x_lo: 2; x = x_hi * 2 + x_lo), y: 4, z: 8, core: 2. Of those that a mesh axis runs over, the one named last changes fastest.
Arguments:
- signal: bfloat16 [32, 4096, 256], P('stn', 'tm'), may hold values from -8 to 8
- cotangent: bfloat16 [32, 4096, 256], P('stn', 'tm'), may hold values from -6 to 6
- window_query: bfloat16 [256, 256], replicated, as said below
- window_key: bfloat16 [256, 256], replicated, as said below
- window_value: bfloat16 [256, 256], replicated, may hold values from -0.375 to 0.375
- window_out: bfloat16 [256, 256], replicated, may hold values from -0.375 to 0.375
- station_query: bfloat16 [256, 256], replicated, as said below
- station_key: bfloat16 [256, 256], replicated, as said below
- station_value: bfloat16 [256, 256], replicated, may hold values from -0.375 to 0.375
- station_out: bfloat16 [256, 256], replicated, may hold values from -0.375 to 0.375
- neighbours: int32 [32, 16], replicated, may hold values from 0 to 31
- neighbour_valid: int32 [32, 16], replicated, may hold values 0 or 1
Outputs:
- block_output: bfloat16 [32, 4096, 256], P('stn', 'tm')
- signal_grad: bfloat16 [32, 4096, 256], P('stn', 'tm')
- grad_window_query: float32 [256, 256], replicated
- grad_window_key: float32 [256, 256], replicated
- grad_window_value: float32 [256, 256], replicated
- grad_window_out: float32 [256, 256], replicated
- grad_station_query: float32 [256, 256], replicated
- grad_station_key: float32 [256, 256], replicated
- grad_station_value: float32 [256, 256], replicated
- grad_station_out: float32 [256, 256], replicated
Inputs may be any that keep to these rules, and one draw needn't show every extreme that they name: `window_query`: a projection scaled by its fan-in. `window_key`: a projection scaled by its fan-in. `station_query`: a projection scaled by its fan-in. `station_key`: a projection scaled by its fan-in.
All inputs are finite; a program needn't handle non-finite values.
Results may differ from a plain program's by a relative error of at most 0.015.
The roundings to bfloat16 on the way count: a program that leaves them out, or rounds other values in their place, can miss the bound.
Values may be sent and summed in bfloat16 or wider, within the bound.
A program may use at most 64 MiB of HBM per device.

v0:
```python
import math

import jax
import jax.numpy as jnp
from jax import lax
from jax.sharding import PartitionSpec as P

HEADS = 4
HALF = 128


def with_halo(cells, sides, width):
    for axis, dim in sides:
        count = lax.axis_size(axis)
        ends = count - 1
        head = lax.slice_in_dim(cells, 0, width, axis=dim)
        tail = lax.slice_in_dim(cells, cells.shape[dim] - width, cells.shape[dim], axis=dim)
        cells = jnp.concatenate(
            [
                lax.ppermute(tail, axis, [(i, (i + 1) % count) for i in range(ends)]),
                cells,
                lax.ppermute(head, axis, [((i + 1) % count, i) for i in range(ends)]),
            ],
            axis=dim,
        )
    return cells


def band_allowed(n_query, n_keys, half_width, first_frame, frames):
    rows = lax.broadcasted_iota(jnp.int32, (n_query, n_keys), 0)
    columns = lax.broadcasted_iota(jnp.int32, (n_query, n_keys), 1)
    offset = columns - rows
    frame_index = columns + first_frame
    return (offset >= 0) & (offset <= 2 * half_width) & (frame_index >= 0) & (frame_index < frames)


def neighbour_counts(neighbours, neighbour_valid, stations):
    targets = lax.broadcasted_iota(jnp.int32, (stations, neighbours.shape[1], stations), 2)
    listed = jnp.where(
        (neighbours[:, :, None] == targets) & (neighbour_valid[:, :, None] == 1), 1.0, 0.0
    )
    diag_rows = lax.broadcasted_iota(jnp.int32, (stations, stations), 0)
    diag_cols = lax.broadcasted_iota(jnp.int32, (stations, stations), 1)
    itself = jnp.where(diag_rows == diag_cols, 1.0, 0.0)
    return (jnp.sum(listed, axis=1) + itself).astype(jnp.float32)


def window_probs(split_q, split_k, allowed, scale):
    scores = (
        jnp.einsum("qhd,khd->hqk", split_q, split_k, preferred_element_type=jnp.float32) * scale
    )
    scores = jnp.where(allowed[None], scores, -1e30)
    highest = jnp.max(scores, axis=-1, keepdims=True)
    raised = jnp.exp(scores - highest)
    return raised / jnp.sum(raised, axis=-1, keepdims=True)


def split_window(queries, kv_rows, heads):
    n_query, width_all = queries.shape
    head_size = width_all // heads
    split_q = queries.reshape(n_query, heads, head_size)
    split_k = kv_rows[:, :width_all].reshape(-1, heads, head_size)
    split_v = kv_rows[:, width_all:].reshape(-1, heads, head_size)
    return (split_q, split_k, split_v, 1.0 / math.sqrt(head_size))


def window_forward(queries, kv_rows, allowed, heads):
    n_query, width_all = queries.shape
    split_q, split_k, split_v, scale = split_window(queries, kv_rows, heads)
    weights = window_probs(split_q, split_k, allowed, scale).astype(jnp.bfloat16)
    mixed = jnp.einsum("hqk,khd->qhd", weights, split_v, preferred_element_type=jnp.float32)
    return mixed.reshape(n_query, width_all).astype(jnp.bfloat16)


def window_backward(queries, kv_rows, allowed, grad_mix, heads):
    n_query, width_all = queries.shape
    split_q, split_k, split_v, scale = split_window(queries, kv_rows, heads)
    scores = (
        jnp.einsum("qhd,khd->hqk", split_q, split_k, preferred_element_type=jnp.float32) * scale
    )
    scores = jnp.where(allowed[None], scores, -1e30)
    highest = jnp.max(scores, axis=-1, keepdims=True)
    raised = jnp.exp(scores - highest)
    totals = jnp.sum(raised, axis=-1, keepdims=True)
    probs = raised / totals
    weights = probs.astype(jnp.bfloat16)
    split_g = grad_mix.reshape(n_query, heads, -1)
    d_probs = jnp.einsum("qhd,khd->hqk", split_g, split_v, preferred_element_type=jnp.float32)
    d_values = jnp.einsum("hqk,qhd->khd", weights, split_g, preferred_element_type=jnp.float32)
    deltas = jnp.sum(probs * d_probs, axis=-1, keepdims=True)
    d_scores = probs * (d_probs - deltas)
    d_scores_b = d_scores.astype(jnp.bfloat16)
    d_queries = (
        jnp.einsum("hqk,khd->qhd", d_scores_b, split_k, preferred_element_type=jnp.float32) * scale
    )
    d_keys = (
        jnp.einsum("hqk,qhd->khd", d_scores_b, split_q, preferred_element_type=jnp.float32) * scale
    )
    n_keys = kv_rows.shape[0]
    d_kv = jnp.concatenate(
        [d_keys.reshape(n_keys, width_all), d_values.reshape(n_keys, width_all)], axis=1
    )
    normalizer = (highest + jnp.log(totals))[:, :, 0]
    row_stats = jnp.concatenate([normalizer.T, deltas[:, :, 0].T], axis=1)
    return (d_queries.reshape(n_query, width_all), d_kv, row_stats)


def station_block(
    rows, grads, counts, station_query, station_key, station_value, station_out, heads
):
    n_sta, n_frm, width_all = rows.shape
    head_size = width_all // heads
    scale = 1.0 / math.sqrt(head_size)
    qkv_weight = jnp.concatenate([station_query, station_key, station_value], axis=1)
    qkv = jnp.dot(rows, qkv_weight, preferred_element_type=jnp.float32).astype(jnp.bfloat16)
    split_q = qkv[..., :width_all].reshape(n_sta, n_frm, heads, head_size)
    split_k = qkv[..., width_all : 2 * width_all].reshape(n_sta, n_frm, heads, head_size)
    split_v = qkv[..., 2 * width_all :].reshape(n_sta, n_frm, heads, head_size)
    scores = (
        jnp.einsum("sfhd,tfhd->fhst", split_q, split_k, preferred_element_type=jnp.float32) * scale
    )
    scores = jnp.where(counts[None, None] > 0.0, scores, -1e30)
    highest = jnp.max(scores, axis=-1, keepdims=True)
    raised = counts[None, None] * jnp.exp(scores - highest)
    probs = raised / jnp.sum(raised, axis=-1, keepdims=True)
    weights = probs.astype(jnp.bfloat16)
    mixed = jnp.einsum("fhst,tfhd->sfhd", weights, split_v, preferred_element_type=jnp.float32)
    mix_narrow = mixed.reshape(n_sta, n_frm, width_all).astype(jnp.bfloat16)
    output = (
        rows.astype(jnp.float32)
        + jnp.dot(mix_narrow, station_out, preferred_element_type=jnp.float32)
    ).astype(jnp.bfloat16)
    grad_out = jnp.einsum("sfd,sfe->de", mix_narrow, grads, preferred_element_type=jnp.float32)
    grad_mix = jnp.dot(grads, station_out.T, preferred_element_type=jnp.float32).astype(
        jnp.bfloat16
    )
    split_g = grad_mix.reshape(n_sta, n_frm, heads, head_size)
    d_probs = jnp.einsum("sfhd,tfhd->fhst", split_g, split_v, preferred_element_type=jnp.float32)
    d_values = jnp.einsum("fhst,sfhd->tfhd", weights, split_g, preferred_element_type=jnp.float32)
    d_scores = probs * (d_probs - jnp.sum(probs * d_probs, axis=-1, keepdims=True))
    d_scores_b = d_scores.astype(jnp.bfloat16)
    d_queries = (
        jnp.einsum("fhst,tfhd->sfhd", d_scores_b, split_k, preferred_element_type=jnp.float32)
        * scale
    )
    d_keys = (
        jnp.einsum("fhst,sfhd->tfhd", d_scores_b, split_q, preferred_element_type=jnp.float32)
        * scale
    )
    d_qkv = jnp.concatenate(
        [
            d_queries.reshape(n_sta, n_frm, width_all),
            d_keys.reshape(n_sta, n_frm, width_all),
            d_values.reshape(n_sta, n_frm, width_all),
        ],
        axis=2,
    ).astype(jnp.bfloat16)
    grad_qkv = jnp.einsum("sfd,sfe->de", rows, d_qkv, preferred_element_type=jnp.float32)
    grad_rows = (
        grads.astype(jnp.float32) + jnp.dot(d_qkv, qkv_weight.T, preferred_element_type=jnp.float32)
    ).astype(jnp.bfloat16)
    return (output, grad_rows, grad_qkv, grad_out)


def body(
    signal,
    cotangent,
    window_query,
    window_key,
    window_value,
    window_out,
    station_query,
    station_key,
    station_value,
    station_out,
    neighbours,
    neighbour_valid,
):
    stn_local, frames_local, width_all = signal.shape
    half_width = HALF
    frames = frames_local * lax.axis_size("tm")
    stations = stn_local * lax.axis_size("stn")
    first_frame = lax.axis_index("tm") * frames_local - half_width
    kv_weight = jnp.concatenate([window_key, window_value], axis=1)
    queries = jnp.dot(signal, window_query, preferred_element_type=jnp.float32).astype(jnp.bfloat16)
    kv_local = jnp.dot(signal, kv_weight, preferred_element_type=jnp.float32).astype(jnp.bfloat16)
    kv_wide = with_halo(kv_local, (("tm", 1),), half_width)
    allowed = band_allowed(
        frames_local, frames_local + 2 * half_width, half_width, first_frame, frames
    )

    def forward_station(operands):
        return window_forward(operands[0], operands[1], allowed, HEADS)

    window_mix = lax.map(forward_station, (queries, kv_wide))
    after_window = (
        signal.astype(jnp.float32)
        + jnp.dot(window_mix, window_out, preferred_element_type=jnp.float32)
    ).astype(jnp.bfloat16)
    frame_rows = lax.all_to_all(after_window, "stn", split_axis=1, concat_axis=0, tiled=True)
    frame_grads = lax.all_to_all(cotangent, "stn", split_axis=1, concat_axis=0, tiled=True)
    counts = neighbour_counts(neighbours, neighbour_valid, stations)
    station_output, station_back, grad_sqkv, grad_so = station_block(
        frame_rows,
        frame_grads,
        counts,
        station_query,
        station_key,
        station_value,
        station_out,
        HEADS,
    )
    block_output = lax.all_to_all(station_output, "stn", split_axis=0, concat_axis=1, tiled=True)
    grad_after = lax.all_to_all(station_back, "stn", split_axis=0, concat_axis=1, tiled=True)
    grad_mix = jnp.dot(grad_after, window_out.T, preferred_element_type=jnp.float32).astype(
        jnp.bfloat16
    )
    grad_wo = jnp.einsum("sfd,sfe->de", window_mix, grad_after, preferred_element_type=jnp.float32)

    def backward_station(operands):
        return window_backward(operands[0], operands[1], allowed, operands[2], HEADS)

    d_query, d_kv_wide, row_stats = lax.map(backward_station, (queries, kv_wide, grad_mix))
    own_kv = d_kv_wide[:, half_width : half_width + frames_local]
    rims = jnp.concatenate(
        [d_kv_wide[:, :half_width], d_kv_wide[:, frames_local + half_width :]], axis=1
    )
    returned = with_halo(rims, (("tm", 1),), half_width)
    own_kv = own_kv.at[:, :half_width].add(returned[:, :half_width])
    own_kv = own_kv.at[:, frames_local - half_width :].add(returned[:, 3 * half_width :])
    d_query_b = d_query.astype(jnp.bfloat16)
    d_kv_b = own_kv.astype(jnp.bfloat16)
    grad_signal = (
        grad_after.astype(jnp.float32)
        + jnp.dot(d_query_b, window_query.T, preferred_element_type=jnp.float32)
        + jnp.dot(d_kv_b, kv_weight.T, preferred_element_type=jnp.float32)
    )
    signal_grad = grad_signal.astype(jnp.bfloat16)
    grad_wq = jnp.einsum("sfd,sfe->de", signal, d_query_b, preferred_element_type=jnp.float32)
    grad_wkv = jnp.einsum("sfd,sfe->de", signal, d_kv_b, preferred_element_type=jnp.float32)
    summed = lax.psum((grad_wq, grad_wkv, grad_wo, grad_sqkv, grad_so), ("stn", "tm"))
    window_sums = (summed[0], summed[1], summed[2])
    station_sums = (summed[3], summed[4])
    factor = 1.0 / math.sqrt(stations * frames)
    sum_wq = window_sums[0] * factor
    sum_wkv = window_sums[1] * factor
    sum_wo = window_sums[2] * factor
    sum_sqkv = station_sums[0] * factor
    sum_so = station_sums[1] * factor
    return (
        block_output,
        signal_grad,
        sum_wq,
        sum_wkv[:, :width_all],
        sum_wkv[:, width_all:],
        sum_wo,
        sum_sqkv[:, :width_all],
        sum_sqkv[:, width_all : 2 * width_all],
        sum_sqkv[:, 2 * width_all :],
        sum_so,
    )


def solution(mesh):
    placed = (
        P("stn", "tm", None),
        P("stn", "tm", None),
        P(),
        P(),
        P(),
        P(),
        P(),
        P(),
        P(),
        P(),
        P(),
        P(),
    )
    return jax.shard_map(
        body,
        mesh=mesh,
        in_specs=placed,
        out_specs=(
            P("stn", "tm", None),
            P("stn", "tm", None),
            P(),
            P(),
            P(),
            P(),
            P(),
            P(),
            P(),
            P(),
        ),
        check_vma=False,
    )
```

profile of v0, /device:TPU:1, one launch (start us, length us, event | category | flops | bytes accessed | tf_op | source)
XLA Modules:
  0.0 432.9 jit_solution(967413305099338172)
XLA Ops:
  7.2 2.0 copy.148
  9.2 8.4 %all-to-all-start.2 = ((bf16[2,256,256]{2,0,1:T(2,128)(2,1)}), bf16[2,256,256]{2,0,1:T(2,128)(2,1)S(1)}, u32[]{:S(2)}, u32[]{:S(2)}) async-start(bf16[2,256,256]{2,0,1:T(2,128)(2,1)} %copy.148), calls=%async_computation.2 | async-start | bytes 524288 | tf_op jit(solution)/shard_map/all_to_all | solution.py:201
  17.7 1.4 fusion.49
  19.1 2.2 collective-permute-start
  24.6 2.3 collective-permute-done
  26.9 5.3 %collective-permute-done.1 = bf16[2,128,512]{2,1,0:T(8,128)(2,1)} collective-permute-done((bf16[2,128,512]{2,1,0:T(8,128)(2,1)S(1)}, bf16[2,128,512]{2,1,0:T(8,128)(2,1)}, u32[]{:S(2)}, u32[]{:S(2)}) %collective-permute-start.1) | collective-permute-done | bytes 262176 | tf_op jit(solution)/shard_map/ppermute | solution.py:22
  33.7 6.0 %while.26 = (s32[]{:T(128)}, bf16[2,256,256]{1,2,0:T(8,128)(2,1)S(1)}, bf16[2,512,512]{1,2,0:T(8,128)(2,1)S(1)}, bf16[2,256,256]{1,2,0:T(8,128)(2,1)S(1)}, pred[...) while((s32[]{:T(128)}, bf16[2,256,256]{1,2,0:T(8,128)(2,1)S(1)}, ...), condition=%wide.region_3.4_spmd.clone, body=%wide.region_0.3_spmd.clone.sunk | while | flops 206899200 | bytes 4203617 | solution.py:195
  41.0 8.7 %all-to-all-start = ((bf16[2,256,256]{2,0,1:T(2,128)(2,1)}), bf16[2,256,256]{2,0,1:T(2,128)(2,1)S(1)}, u32[]{:S(2)}, u32[]{:S(2)}) async-start(bf16[2,256,256]{2,0,1:T(2,128)(2,1)} %copy.136), calls=%async_computation | async-start | bytes 524288 | tf_op jit(solution)/shard_map/all_to_all | solution.py:200
  51.9 6.5 %all-to-all-done = bf16[2,256,256]{2,0,1:T(2,128)(2,1)S(1)} async-done(((bf16[2,256,256]{2,0,1:T(2,128)(2,1)}), bf16[2,256,256]{2,0,1:T(2,128)(2,1)S(1)}, u32[]{:S(2)}, u32[]{:S(2)}) %all-to-all-start) | async-done | bytes 262176 | tf_op jit(solution)/shard_map/all_to_all | solution.py:200
  60.6 1.6 fusion.44
  64.1 3.2 fusion.51
  67.3 2.1 multiply_reduce_fusion.1
  75.2 2.1 fusion.53
  77.4 4.2 all-to-all-start.3
  83.0 7.4 %all-to-all-done.3 = bf16[32,16,256]{2,1,0:T(8,128)(2,1)S(1)} async-done(((bf16[32,16,256]{2,1,0:T(8,128)(2,1)}), bf16[32,16,256]{2,1,0:T(8,128)(2,1)S(1)}, u32[]{:S(2)}, u32[]{:S(2)}) %all-to-all-start.3) | async-done | bytes 262176 | tf_op jit(solution)/shard_map/all_to_all | solution.py:214
  91.4 27.6 %while.27 = (s32[]{:T(128)}, bf16[2,256,256]{1,2,0:T(8,128)(2,1)}, f32[2,512,512]{1,2,0:T(8,128)}, bf16[2,512,512]{1,2,0:T(8,128)(2,1)S(1)}, bf16[2,256,256]{1,2...) while((s32[]{:T(128)}, bf16[2,256,256]{1,2,0:T(8,128)(2,1)}, ...), condition=%wide.region_12.13_spmd.clone, body=%wide.region_8.12_spmd.clone.sunk | while | flops 412353536 | bytes 47867280 | solution.py:223
  94.5 2.0 fusion.181
  96.4 2.9 fusion.182
  99.3 1.6 multiply_reduce_fusion.3
  103.9 1.3 copy-done.10
  108.2 1.9 fusion.181
  110.2 2.9 fusion.182
  113.1 1.6 multiply_reduce_fusion.3
  117.6 1.3 copy-done.10
  119.0 2.1 fusion.89
  121.1 3.9 collective-permute-start.2
  125.0 2.2 fusion.50
  128.9 1.3 slice.105
  133.5 1.9 collective-permute-done.2
  136.5 10.2 %collective-permute-done.3 = f32[2,128,512]{1,2,0:T(8,128)S(1)} collective-permute-done((f32[2,128,512]{1,2,0:T(8,128)S(1)}, f32[2,128,512]{1,2,0:T(8,128)S(1)}, u32[]{:S(2)}, u32[]{:S(2)}) %collective-permute-start.3) | collective-permute-done | bytes 524320 | tf_op jit(solution)/shard_map/ppermute | solution.py:22
  148.2 15.0 %all_to_all.72 = bf16[32,16,256]{2,1,0:T(8,128)(2,1)S(1)} all-to-all(bf16[32,16,256]{2,1,0:T(8,128)(2,1)S(1)} %fusion.55), channel_id=1, replica_groups=mesh['stn'=16,'tm'=16] {'stn'}, dimensions={0} | all-to-all | bytes 524288 | tf_op jit(solution)/shard_map/all_to_all | solution.py:213
  165.3 253.4 %all-reduce.3.cloned.1.call-done = (f32[256,256]{0,1:T(8,128)}, f32[256,512]{0,1:T(8,128)}, f32[256,256]{0,1:T(8,128)}, f32[256,768]{1,0:T(8,128)}, f32[256,256]{0,1:T(8,128)}) async-done(((f32[256,256]{0,1:T(8,128)}, f32[256,512]{0,1:T(8,128)}, f32[256,256]{0,1:T(8,128)}, f32[256,768]{1,0:T(8,128)}, f32[256,256]{0,1:T(8,128)}), (f32[256,256]{0,1:T(8,128)}, f32[256,512]{0,1:T(8,128)}, f32[256,256]{0,1:T(8,128)}, ...) | async-done | bytes 2097168 | tf_op jit(solution)/shard_map/psum | solution.py:241
  (225 shorter events, 54.8 us)
Async XLA Ops:
  7.2 32.6 %copy-start = (bf16[256,256]{1,0:T(8,128)(2,1)S(1)}, bf16[256,256]{1,0:T(8,128)(2,1)}, u32[]{:S(2)}) copy-start(bf16[256,256]{1,0:T(8,128)(2,1)} %param.25) | copy-start | bytes 393220
  7.2 15.7 %copy-start.5 = (bf16[2,256,256]{2,1,0:T(8,128)(2,1)S(1)}, bf16[2,256,256]{2,1,0:T(8,128)(2,1)}, u32[]{:S(2)}) copy-start(bf16[2,256,256]{2,1,0:T(8,128)(2,1)} %param.20) | copy-start | bytes 786436
  7.2 15.4 %copy-start.45 = (s32[32,16]{0,1:T(8,128)S(1)}, s32[32,16]{0,1:T(8,128)}, u32[]{:S(2)}) copy-start(s32[32,16]{0,1:T(8,128)} %param.31) | copy-start | bytes 6148
  7.2 15.6 %copy-start.44 = (s32[32,16]{0,1:T(8,128)S(1)}, s32[32,16]{0,1:T(8,128)}, u32[]{:S(2)}) copy-start(s32[32,16]{0,1:T(8,128)} %param.30) | copy-start | bytes 6148
  7.2 15.6 %copy-start.29 = (bf16[256,256]{1,0:T(8,128)(2,1)S(1)}, bf16[256,256]{1,0:T(8,128)(2,1)}, u32[]{:S(2)}) copy-start(bf16[256,256]{1,0:T(8,128)(2,1)} %param.22) | copy-start | bytes 393220
  9.2 31.8 %all-to-all-start.2 = ((bf16[2,256,256]{2,0,1:T(2,128)(2,1)}), bf16[2,256,256]{2,0,1:T(2,128)(2,1)S(1)}, u32[]{:S(2)}, u32[]{:S(2)}) async-start(bf16[2,256,256]{2,0,1:T(2,128)(2,1)} %copy.148), calls=%async_computation.2 | async-start | bytes 524288 | tf_op jit(solution)/shard_map/all_to_all | solution.py:201
  19.1 7.8 %collective-permute-start = (bf16[2,128,512]{2,1,0:T(8,128)(2,1)S(1)}, bf16[2,128,512]{2,1,0:T(8,128)(2,1)S(1)}, u32[]{:S(2)}, u32[]{:S(2)}) collective-permute-start(bf16[2,128,512]{2,1,0:T(8,128)(2,1)S(1)} %get-tuple-element.285), channel_id=1, source_target_pairs={{0,1},{1,2},{2,3},{3,4},{4,5},{5,6},{6,7},{7,8},{8,9},{9,10},{10,1... | collective-permute-start | bytes 786440 | tf_op jit(solution)/shard_map/ppermute | solution.py:20
  21.3 10.8 %collective-permute-start.1 = (bf16[2,128,512]{2,1,0:T(8,128)(2,1)S(1)}, bf16[2,128,512]{2,1,0:T(8,128)(2,1)}, u32[]{:S(2)}, u32[]{:S(2)}) collective-permute-start(bf16[2,128,512]{2,1,0:T(8,128)(2,1)S(1)} %get-tuple-element.286), channel_id=1, source_target_pairs={{1,0},{2,1},{3,2},{4,3},{5,4},{6,5},{7,6},{8,7},{9,8},{10,9},{11,1... | collective-permute-start | bytes 786440 | tf_op jit(solution)/shard_map/ppermute | solution.py:22
  33.7 16.1 %copy-start.41 = (f32[32,32]{1,0:T(8,128)S(1)}, f32[32,32]{1,0:T(8,128)}, u32[]{:S(2)}) copy-start(f32[32,32]{1,0:T(8,128)} %select_add_fusion) | copy-start | bytes 12292
  39.7 18.8 %copy-start.17 = (bf16[2,256,256]{1,2,0:T(8,128)(2,1)}, bf16[2,256,256]{1,2,0:T(8,128)(2,1)S(1)}, u32[]{:S(2)}) copy-start(bf16[2,256,256]{1,2,0:T(8,128)(2,1)S(1)} %get-tuple-element.99) | copy-start | bytes 786436
  39.7 10.9 %copy-start.27 = (bf16[256,256]{1,0:T(8,128)(2,1)S(1)}, bf16[256,256]{1,0:T(8,128)(2,1)}, u32[]{:S(2)}) copy-start(bf16[256,256]{1,0:T(8,128)(2,1)} %param.29) | copy-start | bytes 393220
  39.8 18.8 %copy-start.46 = (bf16[256,256]{1,0:T(8,128)(2,1)S(1)}, bf16[256,256]{1,0:T(8,128)(2,1)}, u32[]{:S(2)}) copy-start(bf16[256,256]{1,0:T(8,128)(2,1)} %param.28) | copy-start | bytes 393220
  39.8 18.8 %copy-start.47 = (bf16[256,256]{1,0:T(8,128)(2,1)S(1)}, bf16[256,256]{1,0:T(8,128)(2,1)}, u32[]{:S(2)}) copy-start(bf16[256,256]{1,0:T(8,128)(2,1)} %param.27) | copy-start | bytes 393220
  39.8 18.8 %copy-start.48 = (bf16[256,256]{1,0:T(8,128)(2,1)S(1)}, bf16[256,256]{1,0:T(8,128)(2,1)}, u32[]{:S(2)}) copy-start(bf16[256,256]{1,0:T(8,128)(2,1)} %param.26) | copy-start | bytes 393220
  41.0 17.4 %all-to-all-start = ((bf16[2,256,256]{2,0,1:T(2,128)(2,1)}), bf16[2,256,256]{2,0,1:T(2,128)(2,1)S(1)}, u32[]{:S(2)}, u32[]{:S(2)}) async-start(bf16[2,256,256]{2,0,1:T(2,128)(2,1)} %copy.136), calls=%async_computation | async-start | bytes 524288 | tf_op jit(solution)/shard_map/all_to_all | solution.py:200
  49.9 14.2 %copy-start.39 = (f32[32,32]{0,1:T(8,128)}, f32[32,32]{0,1:T(8,128)S(1)}, u32[]{:S(2)}) copy-start(f32[32,32]{0,1:T(8,128)S(1)} %copy.140) | copy-start | bytes 12292
  50.6 24.6 %copy-start.13 = (bf16[2,16,16,256]{3,2,0,1:T(8,128)(2,1)}, bf16[2,16,16,256]{3,2,0,1:T(8,128)(2,1)S(1)}, u32[]{:S(2)}) copy-start(bf16[2,16,16,256]{3,2,0,1:T(8,128)(2,1)S(1)} %copy.149) | copy-start | bytes 786436
  58.5 23.2 %copy-start.19 = (bf16[2,16,16,256]{3,2,0,1:T(8,128)(2,1)}, bf16[2,16,16,256]{3,2,0,1:T(8,128)(2,1)S(1)}, u32[]{:S(2)}) copy-start(bf16[2,16,16,256]{3,2,0,1:T(8,128)(2,1)S(1)} %copy.137) | copy-start | bytes 786436
  77.4 13.0 %all-to-all-start.3 = ((bf16[32,16,256]{2,1,0:T(8,128)(2,1)}), bf16[32,16,256]{2,1,0:T(8,128)(2,1)S(1)}, u32[]{:S(2)}, u32[]{:S(2)}) async-start(bf16[32,16,256]{2,1,0:T(8,128)(2,1)} %fusion.53), calls=%async_computation.3 | async-start | bytes 524288 | tf_op jit(solution)/shard_map/all_to_all | solution.py:214
  81.6 9.8 %copy-start.42 = (pred[512]{0:T(512)(128)(4,1)S(1)}, pred[512]{0:T(512)(128)(4,1)}, u32[]{:S(2)}) copy-start(pred[512]{0:T(512)(128)(4,1)} %get-tuple-element.476) | copy-start | bytes 1540
  81.6 9.8 %copy-start.43 = (pred[512]{0:T(512)(128)(4,1)S(1)}, pred[512]{0:T(512)(128)(4,1)}, u32[]{:S(2)}) copy-start(pred[512]{0:T(512)(128)(4,1)} %get-tuple-element.477) | copy-start | bytes 1540
  81.6 337.1 %all-reduce.3.cloned.1.call-start = ((), (), s32[]{:S(2)}) async-start(), calls=%async_computation.4 | async-start | bytes 4194304 | tf_op jit(solution)/shard_map/psum | solution.py:241
  119.0 6.0 %copy-start.31 = (bf16[32,16,4,64]{3,2,1,0:T(4,128)(2,1)S(1)}, bf16[32,16,4,64]{3,2,1,0:T(4,128)(2,1)}, u32[]{:S(2)}) copy-start(bf16[32,16,4,64]{3,2,1,0:T(4,128)(2,1)} %reshape.182) | copy-start | bytes 786436
  119.0 6.0 %copy-start.38 = (f32[16,4,32]{2,1,0:T(4,128)S(1)}, f32[16,4,32]{2,1,0:T(4,128)}, u32[]{:S(2)}) copy-start(f32[16,4,32]{2,1,0:T(4,128)} %get-tuple-element.287) | copy-start | bytes 24580
  119.0 6.0 %copy-start.40 = (f32[32,32]{0,1:T(8,128)S(1)}, f32[32,32]{0,1:T(8,128)}, u32[]{:S(2)}) copy-start(f32[32,32]{0,1:T(8,128)} %copy-done.39) | copy-start | bytes 12292
  121.1 6.8 %copy-start.14 = (bf16[2,16,16,256]{3,2,0,1:T(8,128)(2,1)S(1)}, bf16[2,16,16,256]{3,2,0,1:T(8,128)(2,1)}, u32[]{:S(2)}) copy-start(bf16[2,16,16,256]{3,2,0,1:T(8,128)(2,1)} %copy-done.13) | copy-start | bytes 786436
  121.1 14.2 %collective-permute-start.2 = (f32[2,128,512]{1,2,0:T(8,128)}, f32[2,128,512]{1,2,0:T(8,128)S(1)}, u32[]{:S(2)}, u32[]{:S(2)}) collective-permute-start(f32[2,128,512]{1,2,0:T(8,128)} %get-tuple-element.276), channel_id=1, source_target_pairs={{0,1},{1,2},{2,3},{3,4},{4,5},{5,6},{6,7},{7,8},{8,9},{9,10},{10,1... | collective-permute-start | bytes 1572872 | tf_op jit(solution)/shard_map/ppermute | solution.py:20
  127.6 5.0 %copy-start.6 = (bf16[2,256,256]{2,1,0:T(8,128)(2,1)S(1)}, bf16[2,256,256]{2,1,0:T(8,128)(2,1)}, u32[]{:S(2)}) copy-start(bf16[2,256,256]{2,1,0:T(8,128)(2,1)} %param.20) | copy-start | bytes 786436
  130.2 16.4 %collective-permute-start.3 = (f32[2,128,512]{1,2,0:T(8,128)S(1)}, f32[2,128,512]{1,2,0:T(8,128)S(1)}, u32[]{:S(2)}, u32[]{:S(2)}) collective-permute-start(f32[2,128,512]{1,2,0:T(8,128)S(1)} %get-tuple-element.275), channel_id=1, source_target_pairs={{1,0},{2,1},{3,2},{4,3},{5,4},{6,5},{7,6},{8,7},{9,8},{10,9},{11,1... | collective-permute-start | bytes 1572872 | tf_op jit(solution)/shard_map/ppermute | solution.py:22
  147.9 16.1 %copy-start.30 = (bf16[256,256]{1,0:T(8,128)(2,1)S(1)}, bf16[256,256]{1,0:T(8,128)(2,1)}, u32[]{:S(2)}) copy-start(bf16[256,256]{1,0:T(8,128)(2,1)} %param.22) | copy-start | bytes 393220
  148.0 16.3 %copy-start.34 = (bf16[256,256]{1,0:T(8,128)(2,1)S(1)}, bf16[256,256]{1,0:T(8,128)(2,1)}, u32[]{:S(2)}) copy-start(bf16[256,256]{1,0:T(8,128)(2,1)} %param.24) | copy-start | bytes 393220
  148.0 16.3 %copy-start.35 = (bf16[256,256]{1,0:T(8,128)(2,1)S(1)}, bf16[256,256]{1,0:T(8,128)(2,1)}, u32[]{:S(2)}) copy-start(bf16[256,256]{1,0:T(8,128)(2,1)} %param.23) | copy-start | bytes 393220
  (35 other events, 72.9 us)
Sparse Core Ops, SparseCore 0:
  148.1 270.5 all-reduce.2
where the time goes:
time: 434 us; the launch traced here: 433 us
  waiting for transfers between devices  287 us (66%)
  matrix products  40.2 us (9%)
  local copies, waits for them, and re-layouts  34.3 us (8%)
  starting transfers between devices  30.1 us (7%)
  blocking collectives  15 us (3%)
  between operations  14.8 us (3%)
  other arithmetic  11.1 us (3%)
    psum x1, waiting for transfers between devices, body(): lax.psum((grad_wq, grad_wkv, grad_wo, grad_sqkv, grad_so), ('stn', 'tm'))  253 us
    ppermute x2, waiting for transfers between devices, with_halo(): lax.ppermute(head, axis, [((i + 1) % count, i) for i in range(ends)])  15.5 us
    all_to_all x1, blocking collectives, body(): lax.all_to_all(station_output, 'stn', split_axis=0, concat_axis=1, tiled=...  15 us
    unnamed x89, local copies, waits for them, and re-layouts  10 us
    all_to_all x1, starting transfers between devices, body(): lax.all_to_all(after_window, 'stn', split_axis=1, concat_axis=0, tiled=True)  8.73 us
  transfers between devices with their start and end apart: 8, of which 7 were waited for; matrix products, arithmetic and copies ran while one was open for 6% of the time, Pallas kernels for 0%

commit v1 on v0

--- a/solution.py
+++ b/solution.py
@@ -1,9 +1,15 @@
+import functools
 import math
 
 import jax
 import jax.numpy as jnp
 from jax import lax
+from jax.experimental import pallas as pl
+from jax.experimental.pallas import tpu as pltpu
 from jax.sharding import PartitionSpec as P
+
+MESH = pl.DeviceIdType.MESH
+LANES = 128
 
 HEADS = 4
 HALF = 128
@@ -160,6 +166,148 @@
         grads.astype(jnp.float32) + jnp.dot(d_qkv, qkv_weight.T, preferred_element_type=jnp.float32)
     ).astype(jnp.bfloat16)
     return (output, grad_rows, grad_qkv, grad_out)
+
+
+def place():
+    stn = lax.axis_index("stn")
+    tm = lax.axis_index("tm")
+    core = stn % 2
+    x = (stn // 2 % 2) * 2 + tm % 2
+    return (stn // 4, x, tm // 2, core)
+
+
+def device_at(y, x, z, core):
+    return ((y * 2 + x // 2) * 2 + core, z * 2 + x % 2)
+
+
+def sum_kernel(
+    wq, wkv, wo, sqkv, so,
+    o_wq, o_wk, o_wv, o_wo, o_sq, o_sk, o_sv, o_so,
+    pack, final, from_core, half, from_plane, part, from_line,
+    core_sem, plane_send, plane_recv, line_send, line_recv,
+    back_core_sem, back_plane_send, back_plane_recv, back_line_send, back_line_recv,
+    factor=1.0,
+):
+    y, x, z, core = place()
+    other = device_at(y, x, z, 1 - core)
+    plane_steps = [(dy, dx) for dy in range(4) for dx in range(4) if dy + dx > 0]
+    plane_ids = [device_at((y + dy) % 4, (x + dx) % 4, z, core) for dy, dx in plane_steps]
+    line_ids = [device_at(y, x, (z + dz) % 8, core) for dz in range(1, 8)]
+    barrier = pltpu.get_barrier_semaphore()
+    for peer in [other] + plane_ids + line_ids:
+        pl.semaphore_signal(barrier, inc=1, device_id=peer, device_id_type=MESH)
+
+    def send(src, dst, send_sem, recv_sem, peer):
+        copy = pltpu.make_async_remote_copy(
+            src_ref=src, dst_ref=dst, send_sem=send_sem, recv_sem=recv_sem,
+            device_id=peer, device_id_type=MESH,
+        )
+        copy.start()
+        return copy
+
+    slabs = [(wq, 0), (wkv, 0), (wkv, 256), (wo, 0), (sqkv, 0), (sqkv, 256), (sqkv, 512), (so, 0)]
+    for i, (ref, first) in enumerate(slabs):
+        for j in range(2):
+            pack[pl.ds((2 * i + j) * 256, 256), :] = ref[
+                :, first + j * LANES : first + (j + 1) * LANES
+            ].astype(jnp.bfloat16)
+    pl.semaphore_wait(barrier, 1 + len(plane_ids) + len(line_ids))
+
+    own_half = pl.multiple_of(core * 2048, 2048)
+    other_half = pl.multiple_of((1 - core) * 2048, 2048)
+    copy = send(
+        pack.at[pl.ds(other_half, 2048)], from_core, core_sem.at[0], core_sem.at[1], other
+    )
+    copy.wait()
+    half[...] = (
+        pack[pl.ds(own_half, 2048), :].astype(jnp.float32) + from_core[...].astype(jnp.float32)
+    ).astype(jnp.bfloat16)
+
+    copies = []
+    for k, (dy, dx) in enumerate(plane_steps):
+        to = ((y + dy) % 4) * 4 + (x + dx) % 4
+        copies.append(
+            send(
+                half.at[pl.ds(pl.multiple_of(to * 128, 128), 128)],
+                from_plane.at[k],
+                plane_send.at[k],
+                plane_recv.at[k],
+                plane_ids[k],
+            )
+        )
+    mine = pl.multiple_of((y * 4 + x) * 128, 128)
+    total = half[pl.ds(mine, 128), :].astype(jnp.float32)
+    for k, copy in enumerate(copies):
+        copy.wait_recv()
+        total = total + from_plane[k].astype(jnp.float32)
+    part[...] = total.astype(jnp.bfloat16)
+    lines = []
+    for k in range(7):
+        to = (z + k + 1) % 8
+        lines.append(
+            send(
+                part.at[pl.ds(pl.multiple_of(to * 16, 16), 16)],
+                from_line.at[k],
+                line_send.at[k],
+                line_recv.at[k],
+                line_ids[k],
+            )
+        )
+    small = part[pl.ds(pl.multiple_of(z * 16, 16), 16), :].astype(jnp.float32)
+    for k, copy in enumerate(lines):
+        copy.wait_recv()
+        small = small + from_line[k].astype(jnp.float32)
+    base = pl.multiple_of(own_half + mine, 128)
+    here = pl.ds(pl.multiple_of(base + z * 16, 16), 16)
+    for copy in [*copies, *lines]:
+        copy.wait_send()
+    final[here, :] = small.astype(jnp.bfloat16)
+    backs = [
+        send(final.at[here], final.at[here], back_line_send.at[k], back_line_recv.at[k], line_ids[k])
+        for k in range(7)
+    ]
+    for copy in backs:
+        copy.wait()
+    rows = pl.ds(base, 128)
+    backs = [
+        send(
+            final.at[rows], final.at[rows], back_plane_send.at[k], back_plane_recv.at[k], plane_ids[k]
+        )
+        for k in range(15)
+    ]
+    for copy in backs:
+        copy.wait()
+    rows = pl.ds(own_half, 2048)
+    send(final.at[rows], final.at[rows], back_core_sem.at[0], back_core_sem.at[1], other).wait()
+    for i, ref in enumerate((o_wq, o_wk, o_wv, o_wo, o_sq, o_sk, o_sv, o_so)):
+        for j in range(2):
+            ref[:, j * LANES : (j + 1) * LANES] = (
+                final[pl.ds((2 * i + j) * 256, 256), :].astype(jnp.float32) * factor
+            )
+
+
+def sum_gradients(wq, wkv, wo, sqkv, so, factor):
+    dma = pltpu.SemaphoreType.DMA
+    vmem = pl.BlockSpec(memory_space=pltpu.VMEM)
+    return pl.pallas_call(
+        functools.partial(sum_kernel, factor=factor),
+        out_shape=[jax.ShapeDtypeStruct((256, 256), jnp.float32)] * 8,
+        in_specs=[vmem] * 5,
+        out_specs=[vmem] * 8,
+        scratch_shapes=[
+            pltpu.VMEM((4096, LANES), jnp.bfloat16),
+            pltpu.VMEM((4096, LANES), jnp.bfloat16),
+            pltpu.VMEM((2048, LANES), jnp.bfloat16),
+            pltpu.VMEM((2048, LANES), jnp.bfloat16),
+            pltpu.VMEM((15, 128, LANES), jnp.bfloat16),
+            pltpu.VMEM((128, LANES), jnp.bfloat16),
+            pltpu.VMEM((7, 16, LANES), jnp.bfloat16),
+            dma((2,)), dma((15,)), dma((15,)), dma((7,)), dma((7,)),
+            dma((2,)), dma((15,)), dma((15,)), dma((7,)), dma((7,)),
+        ],
+        compiler_params=pltpu.CompilerParams(collective_id=0, has_side_effects=True),
+        name="sum_gradients",
+    )(wq, wkv, wo, sqkv, so)
 
 
 def body(
@@ -238,27 +386,9 @@
     signal_grad = grad_signal.astype(jnp.bfloat16)
     grad_wq = jnp.einsum("sfd,sfe->de", signal, d_query_b, preferred_element_type=jnp.float32)
     grad_wkv = jnp.einsum("sfd,sfe->de", signal, d_kv_b, preferred_element_type=jnp.float32)
-    summed = lax.psum((grad_wq, grad_wkv, grad_wo, grad_sqkv, grad_so), ("stn", "tm"))
-    window_sums = (summed[0], summed[1], summed[2])
-    station_sums = (summed[3], summed[4])
     factor = 1.0 / math.sqrt(stations * frames)
-    sum_wq = window_sums[0] * factor
-    sum_wkv = window_sums[1] * factor
-    sum_wo = window_sums[2] * factor
-    sum_sqkv = station_sums[0] * factor
-    sum_so = station_sums[1] * factor
-    return (
-        block_output,
-        signal_grad,
-        sum_wq,
-        sum_wkv[:, :width_all],
-        sum_wkv[:, width_all:],
-        sum_wo,
-        sum_sqkv[:, :width_all],
-        sum_sqkv[:, width_all : 2 * width_all],
-        sum_sqkv[:, 2 * width_all :],
-        sum_so,
-    )
+    sums = sum_gradients(grad_wq, grad_wkv, grad_wo, grad_sqkv, grad_so, factor)
+    return (block_output, signal_grad, *sums)
 
 
 def solution(mesh):

time: 434 us -> 210 us (0.48)
  waiting for transfers between devices: 287 us -> 40.1 us
  Pallas kernels: 0 us -> 43.6 us
  blocking collectives: 15 us -> 0 us
  between operations: 14.8 us -> 1.33 us
  starting transfers between devices: 30.1 us -> 35.5 us
    psum x1 -> x0, waiting for transfers between devices: 253 us -> none  [body(): lax.psum((grad_wq, grad_wkv, grad_wo, grad_sqkv, grad_so), ('stn', 'tm'))]
    pallas_call x0 -> x1, Pallas kernels: none -> 43.6 us  [sum_gradients(): pl.pallas_call(functools.partial(sum_kernel, factor=factor), out_shape=[j...]
    ppermute x2, waiting for transfers between devices: 4.2 us -> 20.4 us  [with_halo(): lax.ppermute(tail, axis, [(i, (i + 1) % count) for i in range(ends)])]
    all_to_all x1 -> x0, blocking collectives: 15 us -> none  [body(): lax.all_to_all(station_output, 'stn', split_axis=0, concat_axis=1, tiled=...]
    ppermute x2, waiting for transfers between devices: 15.5 us -> 5.27 us  [with_halo(): lax.ppermute(head, axis, [((i + 1) % count, i) for i in range(ends)])]
    all_to_all x0 -> x1, starting transfers between devices: none -> 4.87 us  [body(): lax.all_to_all(station_output, 'stn', split_axis=0, concat_axis=1, tiled=...]
    unnamed x89 -> x86, local copies, waits for them, and re-layouts: 10 us -> 14.6 us
  transfers between devices with their start and end apart: 8 -> 8, of which waited for: 7 -> 5; matrix products, arithmetic and copies ran while one was open for 6% -> 22% of each run, Pallas kernels for 0% -> 0%
where the time goes in v1:
time: 210 us; the launch traced here: 209 us
  Pallas kernels  43.6 us (21%)
  matrix products  42.7 us (20%)
  waiting for transfers between devices  40.1 us (19%)
  local copies, waits for them, and re-layouts  36.6 us (17%)
  starting transfers between devices  35.5 us (17%)
  other arithmetic  8.98 us (4%)
    pallas_call x1, Pallas kernels, sum_gradients(): pl.pallas_call(functools.partial(sum_kernel, factor=factor), out_shape=[j...  43.6 us
    ppermute x2, waiting for transfers between devices, with_halo(): lax.ppermute(tail, axis, [(i, (i + 1) % count) for i in range(ends)])  20.4 us
    unnamed x86, local copies, waits for them, and re-layouts  14.6 us
    all_to_all x1, starting transfers between devices, body(): lax.all_to_all(after_window, 'stn', split_axis=1, concat_axis=0, tiled=True)  8.74 us
    all_to_all x1, starting transfers between devices, body(): lax.all_to_all(cotangent, 'stn', split_axis=1, concat_axis=0, tiled=True)  8.44 us
    all_to_all x1, waiting for transfers between devices, body(): lax.all_to_all(station_back, 'stn', split_axis=0, concat_axis=1, tiled=True)  7.83 us
    ppermute x2, starting transfers between devices, with_halo(): lax.ppermute(tail, axis, [(i, (i + 1) % count) for i in range(ends)])  6.55 us
    all_to_all x1, waiting for transfers between devices, body(): lax.all_to_all(after_window, 'stn', split_axis=1, concat_axis=0, tiled=True)  6.52 us
  transfers between devices with their start and end apart: 8, of which 5 were waited for; matrix products, arithmetic and copies ran while one was open for 22% of the time, Pallas kernels for 0%

profile of v1, /device:TPU:1, one launch (start us, length us, event | category | flops | bytes accessed | tf_op | source)
XLA Modules:
  0.0 209.2 jit_solution(2232442873561623728)
XLA Ops:
  0.7 2.0 copy.133
  2.7 8.4 %all-to-all-start.2 = ((bf16[2,256,256]{2,0,1:T(2,128)(2,1)}), bf16[2,256,256]{2,0,1:T(2,128)(2,1)S(1)}, u32[]{:S(2)}, u32[]{:S(2)}) async-start(bf16[2,256,256]{2,0,1:T(2,128)(2,1)} %copy.133), calls=%async_computation.2 | async-start | bytes 524288 | tf_op jit(solution)/shard_map/all_to_all | solution.py:349
  12.6 2.2 %collective-permute-start = (bf16[2,128,512]{2,1,0:T(8,128)(2,1)S(1)}, bf16[2,128,512]{2,1,0:T(8,128)(2,1)S(1)}, u32[]{:S(2)}, u32[]{:S(2)}) collective-permute-start(bf16[2,128,512]{2,1,0:T(8,128)(2,1)S(1)} %get-tuple-element.251), channel_id=1, source_target_pairs={{0,1},{1,2},{2,3},{3,4},{4,5},{5,6},{6,7},{7,8},{8,9},{9,10},{10,1... | collective-permute-start | bytes 786440 | tf_op jit(solution)/shard_map/ppermute | solution.py:26
  18.1 2.3 %collective-permute-done = bf16[2,128,512]{2,1,0:T(8,128)(2,1)S(1)} collective-permute-done((bf16[2,128,512]{2,1,0:T(8,128)(2,1)S(1)}, bf16[2,128,512]{2,1,0:T(8,128)(2,1)S(1)}, u32[]{:S(2)}, u32[]{:S(2)}) %collective-permute-start) | collective-permute-done | bytes 262176 | tf_op jit(solution)/shard_map/ppermute | solution.py:26
  20.3 5.3 %collective-permute-done.1 = bf16[2,128,512]{2,1,0:T(8,128)(2,1)} collective-permute-done((bf16[2,128,512]{2,1,0:T(8,128)(2,1)S(1)}, bf16[2,128,512]{2,1,0:T(8,128)(2,1)}, u32[]{:S(2)}, u32[]{:S(2)}) %collective-permute-start.1) | collective-permute-done | bytes 262176 | tf_op jit(solution)/shard_map/ppermute | solution.py:28
  27.2 6.0 %while.26 = (s32[]{:T(128)}, bf16[2,256,256]{1,2,0:T(8,128)(2,1)S(1)}, bf16[2,512,512]{1,2,0:T(8,128)(2,1)S(1)}, bf16[2,256,256]{1,2,0:T(8,128)(2,1)S(1)}, pred[...) while((s32[]{:T(128)}, bf16[2,256,256]{1,2,0:T(8,128)(2,1)S(1)}, ...), condition=%wide.region_3.4_spmd.clone, body=%wide.region_0.3_spmd.clone.sunk | while | flops 206899200 | bytes 4203617 | solution.py:343
  34.6 8.7 %all-to-all-start = ((bf16[2,256,256]{2,0,1:T(2,128)(2,1)}), bf16[2,256,256]{2,0,1:T(2,128)(2,1)S(1)}, u32[]{:S(2)}, u32[]{:S(2)}) async-start(bf16[2,256,256]{2,0,1:T(2,128)(2,1)} %copy.121), calls=%async_computation | async-start | bytes 524288 | tf_op jit(solution)/shard_map/all_to_all | solution.py:348
  45.5 6.5 %all-to-all-done = bf16[2,256,256]{2,0,1:T(2,128)(2,1)S(1)} async-done(((bf16[2,256,256]{2,0,1:T(2,128)(2,1)}), bf16[2,256,256]{2,0,1:T(2,128)(2,1)S(1)}, u32[]{:S(2)}, u32[]{:S(2)}) %all-to-all-start) | async-done | bytes 262176 | tf_op jit(solution)/shard_map/all_to_all | solution.py:348
  57.6 3.2 %fusion.51 = bf16[32,16,4,64]{3,0,2,1:T(8,128)(2,1)} fusion(bf16[32,16,4,64]{3,2,1,0:T(4,128)(2,1)} %reshape.185, f32[16,4,32]{2,1,0:T(4,128)} %get-tuple-element.253, f32[16,4,32,32]{2,3,1,0:T(8,128)} %copy-done.17, f32[32,32]{0,1:T(8,128)S(1)} %copy.125), kind=kOutput, calls=%fused_computation.76 | convolution fusion | flops 8783903 | bytes 798720 | tf_op jit(solution)/shard_map/fhst,sfhd->tfhd/dot_general | solution.py:145
  60.8 3.2 %fusion.50 = bf16[32,16,4,64]{3,0,2,1:T(8,128)(2,1)} fusion(bf16[32,16,4,64]{3,2,1,0:T(4,128)(2,1)} %reshape.182, f32[16,4,32]{2,1,0:T(4,128)} %get-tuple-element.253, f32[16,4,32,32]{2,3,1,0:T(8,128)} %copy-done.17, f32[32,32]{0,1:T(8,128)S(1)} %copy.125), kind=kOutput, calls=%fused_computation.75 | convolution fusion | flops 8783903 | bytes 798720 | tf_op jit(solution)/shard_map/fhst,tfhd->sfhd/dot_general | solution.py:133
  64.0 2.1 multiply_reduce_fusion.1
  69.8 2.0 fusion.53
  74.7 4.4 %all-to-all-start.3 = ((bf16[32,16,256]{2,1,0:T(8,128)(2,1)}), bf16[32,16,256]{2,1,0:T(8,128)(2,1)S(1)}, u32[]{:S(2)}, u32[]{:S(2)}) async-start(bf16[32,16,256]{2,1,0:T(8,128)(2,1)} %fusion.53), calls=%async_computation.3 | async-start | bytes 524288 | tf_op jit(solution)/shard_map/all_to_all | solution.py:362
  80.0 7.8 %all-to-all-done.3 = bf16[32,16,256]{2,1,0:T(8,128)(2,1)S(1)} async-done(((bf16[32,16,256]{2,1,0:T(8,128)(2,1)}), bf16[32,16,256]{2,1,0:T(8,128)(2,1)S(1)}, u32[]{:S(2)}, u32[]{:S(2)}) %all-to-all-start.3) | async-done | bytes 262176 | tf_op jit(solution)/shard_map/all_to_all | solution.py:362
  87.8 4.9 %all-to-all-start.1 = ((bf16[32,16,256]{2,1,0:T(8,128)(2,1)}), bf16[32,16,256]{2,1,0:T(8,128)(2,1)}, u32[]{:S(2)}, u32[]{:S(2)}) async-start(bf16[32,16,256]{2,1,0:T(8,128)(2,1)} %fusion.55), calls=%async_computation.1 | async-start | bytes 524288 | tf_op jit(solution)/shard_map/all_to_all | solution.py:361
  93.7 27.6 %while.27 = (s32[]{:T(128)}, bf16[2,256,256]{1,2,0:T(8,128)(2,1)}, f32[2,512,512]{1,2,0:T(8,128)}, bf16[2,512,512]{1,2,0:T(8,128)(2,1)S(1)}, bf16[2,256,256]{1,2...) while((s32[]{:T(128)}, bf16[2,256,256]{1,2,0:T(8,128)(2,1)}, ...), condition=%wide.region_12.13_spmd.clone, body=%wide.region_8.12_spmd.clone.sunk | while | flops 412353536 | bytes 47867280 | solution.py:371
  96.7 2.0 fusion.179
  98.7 2.9 %fusion.180 = f32[4,64,512]{2,1,0:T(8,128)} fusion(bf16[256,4,64]{0,2,1:T(8,128)(2,1)} %bitcast.205, f32[4,256]{1,0:T(4,128)S(1)} %get-tuple-element.357, pred[256,512]{1,0:T(8,128)(4,1)} %fusion.178, bf16[256,4,64]{0,2,1:T(8,128)(2,1)} %bitcast.195, bf16[512,4,64]{0,2,1:T(8,128)(2,1)S(1)} %bitcast.191), kind=kOutput, calls=%fused_computation.36.clone.1 | convolution fusion | flops 136840704 | bytes 1183744 | tf_op jit(solution)/shard_map/while/body/eval_jaxpr/hqk,qhd->khd/dot_general | solution.py:95
  101.6 1.6 multiply_reduce_fusion.3
  110.5 1.9 fusion.179
  112.5 2.9 %fusion.180 = f32[4,64,512]{2,1,0:T(8,128)} fusion(bf16[256,4,64]{0,2,1:T(8,128)(2,1)} %bitcast.205, f32[4,256]{1,0:T(4,128)S(1)} %get-tuple-element.357, pred[256,512]{1,0:T(8,128)(4,1)} %fusion.178, bf16[256,4,64]{0,2,1:T(8,128)(2,1)} %bitcast.195, bf16[512,4,64]{0,2,1:T(8,128)(2,1)S(1)} %bitcast.191), kind=kOutput, calls=%fused_computation.36.clone.1 | convolution fusion | flops 136840704 | bytes 1183744 | tf_op jit(solution)/shard_map/while/body/eval_jaxpr/hqk,qhd->khd/dot_general | solution.py:95
  115.4 1.6 multiply_reduce_fusion.3
  121.3 2.4 %fusion.89 = (f32[2,128,512]{1,2,0:T(8,128)}, f32[2,128,512]{1,2,0:T(8,128)}) fusion(f32[2,512,512]{1,2,0:T(8,128)} %get-tuple-element.109), kind=kLoop, calls=%fused_computation.142 | loop fusion | bytes 2097152 | tf_op jit(solution)/shard_map/slice | solution.py:374
  125.0 4.3 %collective-permute-start.2 = (f32[2,128,512]{1,2,0:T(8,128)}, f32[2,128,512]{1,2,0:T(8,128)S(1)}, u32[]{:S(2)}, u32[]{:S(2)}) collective-permute-start(f32[2,128,512]{1,2,0:T(8,128)} %get-tuple-element.247), channel_id=1, source_target_pairs={{0,1},{1,2},{2,3},{3,4},{4,5},{5,6},{6,7},{7,8},{8,9},{9,10},{10,1... | collective-permute-start | bytes 1572872 | tf_op jit(solution)/shard_map/ppermute | solution.py:26
  129.4 1.9 convolution_bitcast_fusion.3.wo
  132.4 1.7 copy.132
  134.3 18.1 %collective-permute-done.2 = f32[2,128,512]{1,2,0:T(8,128)S(1)} collective-permute-done((f32[2,128,512]{1,2,0:T(8,128)}, f32[2,128,512]{1,2,0:T(8,128)S(1)}, u32[]{:S(2)}, u32[]{:S(2)}) %collective-permute-start.2) | collective-permute-done | bytes 524320 | tf_op jit(solution)/shard_map/ppermute | solution.py:26
  155.9 43.6 %sum_gradients.1 = (f32[256,256]{1,0:T(8,128)}, f32[256,256]{1,0:T(8,128)}, f32[256,256]{1,0:T(8,128)}, f32[256,256]{1,0:T(8,128)}, f32[256,256]{1,0:T(8,128)}, ...) custom-call(f32[256,256]{1,0:T(8,128)} %convolution_bitcast_fusion.4.wq, ...), custom_call_target="tpu_custom_call" | custom-call | tf_op jit(solution)/shard_map/sum_gradients/pallas_call | solution.py:292
  199.6 1.8 copy.216
  201.4 1.7 copy.217
  203.0 1.7 copy.218
  204.7 1.7 copy.219
  (214 shorter events, 52.8 us)
Async XLA Ops:
  0.6 43.5 %copy-start = (bf16[256,256]{1,0:T(8,128)(2,1)S(1)}, bf16[256,256]{1,0:T(8,128)(2,1)}, u32[]{:S(2)}) copy-start(bf16[256,256]{1,0:T(8,128)(2,1)} %param.29) | copy-start | bytes 393220
  0.7 15.6 %copy-start.5 = (bf16[2,256,256]{2,1,0:T(8,128)(2,1)S(1)}, bf16[2,256,256]{2,1,0:T(8,128)(2,1)}, u32[]{:S(2)}) copy-start(bf16[2,256,256]{2,1,0:T(8,128)(2,1)} %param.20) | copy-start | bytes 786436
  0.7 15.4 %copy-start.40 = (s32[32,16]{0,1:T(8,128)S(1)}, s32[32,16]{0,1:T(8,128)}, u32[]{:S(2)}) copy-start(s32[32,16]{0,1:T(8,128)} %param.31) | copy-start | bytes 6148
  0.7 15.6 %copy-start.39 = (s32[32,16]{0,1:T(8,128)S(1)}, s32[32,16]{0,1:T(8,128)}, u32[]{:S(2)}) copy-start(s32[32,16]{0,1:T(8,128)} %param.30) | copy-start | bytes 6148
  0.7 15.6 %copy-start.25 = (bf16[256,256]{1,0:T(8,128)(2,1)S(1)}, bf16[256,256]{1,0:T(8,128)(2,1)}, u32[]{:S(2)}) copy-start(bf16[256,256]{1,0:T(8,128)(2,1)} %param.22) | copy-start | bytes 393220
  2.7 31.9 %all-to-all-start.2 = ((bf16[2,256,256]{2,0,1:T(2,128)(2,1)}), bf16[2,256,256]{2,0,1:T(2,128)(2,1)S(1)}, u32[]{:S(2)}, u32[]{:S(2)}) async-start(bf16[2,256,256]{2,0,1:T(2,128)(2,1)} %copy.133), calls=%async_computation.2 | async-start | bytes 524288 | tf_op jit(solution)/shard_map/all_to_all | solution.py:349
  12.6 7.8 %collective-permute-start = (bf16[2,128,512]{2,1,0:T(8,128)(2,1)S(1)}, bf16[2,128,512]{2,1,0:T(8,128)(2,1)S(1)}, u32[]{:S(2)}, u32[]{:S(2)}) collective-permute-start(bf16[2,128,512]{2,1,0:T(8,128)(2,1)S(1)} %get-tuple-element.251), channel_id=1, source_target_pairs={{0,1},{1,2},{2,3},{3,4},{4,5},{5,6},{6,7},{7,8},{8,9},{9,10},{10,1... | collective-permute-start | bytes 786440 | tf_op jit(solution)/shard_map/ppermute | solution.py:26
  14.8 10.8 %collective-permute-start.1 = (bf16[2,128,512]{2,1,0:T(8,128)(2,1)S(1)}, bf16[2,128,512]{2,1,0:T(8,128)(2,1)}, u32[]{:S(2)}, u32[]{:S(2)}) collective-permute-start(bf16[2,128,512]{2,1,0:T(8,128)(2,1)S(1)} %get-tuple-element.252), channel_id=1, source_target_pairs={{1,0},{2,1},{3,2},{4,3},{5,4},{6,5},{7,6},{8,7},{9,8},{10,9},{11,1... | collective-permute-start | bytes 786440 | tf_op jit(solution)/shard_map/ppermute | solution.py:28
  27.2 16.1 %copy-start.36 = (f32[32,32]{1,0:T(8,128)S(1)}, f32[32,32]{1,0:T(8,128)}, u32[]{:S(2)}) copy-start(f32[32,32]{1,0:T(8,128)} %select_add_fusion) | copy-start | bytes 12292
  33.2 18.8 %copy-start.14 = (bf16[2,256,256]{1,2,0:T(8,128)(2,1)}, bf16[2,256,256]{1,2,0:T(8,128)(2,1)S(1)}, u32[]{:S(2)}) copy-start(bf16[2,256,256]{1,2,0:T(8,128)(2,1)S(1)} %get-tuple-element.107) | copy-start | bytes 786436
  33.3 18.8 %copy-start.41 = (bf16[256,256]{1,0:T(8,128)(2,1)S(1)}, bf16[256,256]{1,0:T(8,128)(2,1)}, u32[]{:S(2)}) copy-start(bf16[256,256]{1,0:T(8,128)(2,1)} %param.28) | copy-start | bytes 393220
  33.3 18.8 %copy-start.43 = (bf16[256,256]{1,0:T(8,128)(2,1)S(1)}, bf16[256,256]{1,0:T(8,128)(2,1)}, u32[]{:S(2)}) copy-start(bf16[256,256]{1,0:T(8,128)(2,1)} %param.27) | copy-start | bytes 393220
  33.3 18.8 %copy-start.45 = (bf16[256,256]{1,0:T(8,128)(2,1)S(1)}, bf16[256,256]{1,0:T(8,128)(2,1)}, u32[]{:S(2)}) copy-start(bf16[256,256]{1,0:T(8,128)(2,1)} %param.26) | copy-start | bytes 393220
  34.6 17.4 %all-to-all-start = ((bf16[2,256,256]{2,0,1:T(2,128)(2,1)}), bf16[2,256,256]{2,0,1:T(2,128)(2,1)S(1)}, u32[]{:S(2)}, u32[]{:S(2)}) async-start(bf16[2,256,256]{2,0,1:T(2,128)(2,1)} %copy.121), calls=%async_computation | async-start | bytes 524288 | tf_op jit(solution)/shard_map/all_to_all | solution.py:348
  44.1 8.4 %copy-start.21 = (bf16[2,16,16,256]{3,2,0,1:T(8,128)(2,1)}, bf16[2,16,16,256]{3,2,0,1:T(8,128)(2,1)S(1)}, u32[]{:S(2)}) copy-start(bf16[2,16,16,256]{3,2,0,1:T(8,128)(2,1)S(1)} %copy.134) | copy-start | bytes 786436
  74.7 18.7 %copy-start.24 = (bf16[256,256]{1,0:T(8,128)(2,1)S(1)}, bf16[256,256]{1,0:T(8,128)(2,1)}, u32[]{:S(2)}) copy-start(bf16[256,256]{1,0:T(8,128)(2,1)} %param.25) | copy-start | bytes 393220
  74.7 19.0 %copy-start.37 = (pred[512]{0:T(512)(128)(4,1)S(1)}, pred[512]{0:T(512)(128)(4,1)}, u32[]{:S(2)}) copy-start(pred[512]{0:T(512)(128)(4,1)} %get-tuple-element.439) | copy-start | bytes 1540
  74.7 19.0 %copy-start.38 = (pred[512]{0:T(512)(128)(4,1)S(1)}, pred[512]{0:T(512)(128)(4,1)}, u32[]{:S(2)}) copy-start(pred[512]{0:T(512)(128)(4,1)} %get-tuple-element.440) | copy-start | bytes 1540
  74.7 13.1 %all-to-all-start.3 = ((bf16[32,16,256]{2,1,0:T(8,128)(2,1)}), bf16[32,16,256]{2,1,0:T(8,128)(2,1)S(1)}, u32[]{:S(2)}, u32[]{:S(2)}) async-start(bf16[32,16,256]{2,1,0:T(8,128)(2,1)} %fusion.53), calls=%async_computation.3 | async-start | bytes 524288 | tf_op jit(solution)/shard_map/all_to_all | solution.py:362
  87.8 44.6 %all-to-all-start.1 = ((bf16[32,16,256]{2,1,0:T(8,128)(2,1)}), bf16[32,16,256]{2,1,0:T(8,128)(2,1)}, u32[]{:S(2)}, u32[]{:S(2)}) async-start(bf16[32,16,256]{2,1,0:T(8,128)(2,1)} %fusion.55), calls=%async_computation.1 | async-start | bytes 524288 | tf_op jit(solution)/shard_map/all_to_all | solution.py:361
  121.3 8.1 %copy-start.8 = (bf16[2,16,16,256]{3,2,1,0:T(8,128)(2,1)S(1)}, bf16[2,16,16,256]{3,2,1,0:T(8,128)(2,1)}, u32[]{:S(2)}) copy-start(bf16[2,16,16,256]{3,2,1,0:T(8,128)(2,1)} %copy-done.7) | copy-start | bytes 786436
  121.3 10.0 %copy-start.6 = (bf16[2,256,256]{2,1,0:T(8,128)(2,1)S(1)}, bf16[2,256,256]{2,1,0:T(8,128)(2,1)}, u32[]{:S(2)}) copy-start(bf16[2,256,256]{2,1,0:T(8,128)(2,1)} %param.20) | copy-start | bytes 786436
  121.3 10.0 %copy-start.20 = (bf16[2,256,256]{1,2,0:T(8,128)(2,1)S(1)}, bf16[2,256,256]{1,2,0:T(8,128)(2,1)}, u32[]{:S(2)}) copy-start(bf16[2,256,256]{1,2,0:T(8,128)(2,1)} %get-tuple-element.108) | copy-start | bytes 786436
  121.3 11.0 %copy-start.11 = (f32[2,512,512]{1,2,0:T(8,128)S(1)}, f32[2,512,512]{1,2,0:T(8,128)}, u32[]{:S(2)}) copy-start(f32[2,512,512]{1,2,0:T(8,128)} %get-tuple-element.109) | copy-start | bytes 6291460
  123.7 29.8 %collective-permute-start.3 = (f32[2,128,512]{1,2,0:T(8,128)}, f32[2,128,512]{1,2,0:T(8,128)S(1)}, u32[]{:S(2)}, u32[]{:S(2)}) collective-permute-start(f32[2,128,512]{1,2,0:T(8,128)} %get-tuple-element.246), channel_id=1, source_target_pairs={{1,0},{2,1},{3,2},{4,3},{5,4},{6,5},{7,6},{8,7},{9,8},{10,9},{11,1... | collective-permute-start | bytes 1572872 | tf_op jit(solution)/shard_map/ppermute | solution.py:28
  125.0 9.0 %copy-start.26 = (bf16[256,256]{1,0:T(8,128)(2,1)S(1)}, bf16[256,256]{1,0:T(8,128)(2,1)}, u32[]{:S(2)}) copy-start(bf16[256,256]{1,0:T(8,128)(2,1)} %param.22) | copy-start | bytes 393220
  125.0 27.4 %collective-permute-start.2 = (f32[2,128,512]{1,2,0:T(8,128)}, f32[2,128,512]{1,2,0:T(8,128)S(1)}, u32[]{:S(2)}, u32[]{:S(2)}) collective-permute-start(f32[2,128,512]{1,2,0:T(8,128)} %get-tuple-element.247), channel_id=1, source_target_pairs={{0,1},{1,2},{2,3},{3,4},{4,5},{5,6},{6,7},{7,8},{8,9},{9,10},{10,1... | collective-permute-start | bytes 1572872 | tf_op jit(solution)/shard_map/ppermute | solution.py:26
  134.3 20.5 %copy-start.29 = (bf16[256,256]{1,0:T(8,128)(2,1)S(1)}, bf16[256,256]{1,0:T(8,128)(2,1)}, u32[]{:S(2)}) copy-start(bf16[256,256]{1,0:T(8,128)(2,1)} %param.24) | copy-start | bytes 393220
  134.3 20.5 %copy-start.30 = (bf16[256,256]{1,0:T(8,128)(2,1)S(1)}, bf16[256,256]{1,0:T(8,128)(2,1)}, u32[]{:S(2)}) copy-start(bf16[256,256]{1,0:T(8,128)(2,1)} %param.23) | copy-start | bytes 393220
  199.6 7.5 %copy-start.33 = (f32[256,256]{1,0:T(8,128)S(1)}, f32[256,256]{1,0:T(8,128)}, u32[]{:S(2)}) copy-start(f32[256,256]{1,0:T(8,128)} %get-tuple-element.426) | copy-start | bytes 786436
  199.6 8.2 %copy-start.32 = (f32[256,256]{1,0:T(8,128)S(1)}, f32[256,256]{1,0:T(8,128)}, u32[]{:S(2)}) copy-start(f32[256,256]{1,0:T(8,128)} %get-tuple-element.427) | copy-start | bytes 786436
  199.6 8.9 %copy-start.31 = (f32[256,256]{1,0:T(8,128)S(1)}, f32[256,256]{1,0:T(8,128)}, u32[]{:S(2)}) copy-start(f32[256,256]{1,0:T(8,128)} %get-tuple-element.428) | copy-start | bytes 786436
  (32 other events, 63.4 us)

commit v2 on v0

v2 whole, which is shorter than its diff:
```python
import functools
import math

import jax
import jax.numpy as jnp
from jax import lax
from jax.experimental import pallas as pl
from jax.experimental.pallas import tpu as pltpu
from jax.sharding import PartitionSpec as P

HEADS = 4
HALF = 128
LANES = 128
MESH = pl.DeviceIdType.MESH
F32 = jnp.float32
BF16 = jnp.bfloat16
STN = 16
TM = 16


def dot(a, b, kind="nn"):
    dims = {"nn": ((1,), (0,)), "nt": ((1,), (1,)), "tn": ((0,), (0,))}[kind]
    return lax.dot_general(a, b, (dims, ((), ())), preferred_element_type=F32)


def device_at(y, x, z, core):
    return ((y * 2 + x // 2) * 2 + core, z * 2 + x % 2)


def send(src, dst, send_sem, recv_sem, peer):
    copy = pltpu.make_async_remote_copy(
        src_ref=src,
        dst_ref=dst,
        send_sem=send_sem,
        recv_sem=recv_sem,
        device_id=peer,
        device_id_type=MESH,
    )
    copy.start()
    return copy


class Place:
    def __init__(self):
        self.stn = lax.axis_index("stn")
        self.tm = lax.axis_index("tm")
        self.core = self.stn % 2
        self.x = (self.stn // 2 % 2) * 2 + self.tm % 2
        self.y = self.stn // 4
        self.z = self.tm // 2
        y, x, z, core = self.y, self.x, self.z, self.core
        self.other = device_at(y, x, z, 1 - core)
        self.plane_steps = [(dy, dx) for dy in range(4) for dx in range(4) if dy + dx > 0]
        self.plane_ids = [
            device_at((y + dy) % 4, (x + dx) % 4, z, core) for dy, dx in self.plane_steps
        ]
        self.line_ids = [device_at(y, x, (z + dz) % 8, core) for dz in range(1, 8)]
        self.stn_ids = [((self.stn + r) % STN, self.tm) for r in range(1, STN)]
        self.left = (self.stn, (self.tm + TM - 1) % TM)
        self.right = (self.stn, (self.tm + 1) % TM)
        beside = (self.tm + TM - 1 + 2 * (self.stn // 8)) % TM
        self.rim_ids = [((self.stn + r) % STN, beside) for r in range(STN)]
        self.rim_sources = []
        for r in range(STN):
            source = (self.stn + STN - r) % STN
            self.rim_sources.append((source, (self.tm + TM + 1 - 2 * (source // 8)) % TM))


class Sum:
    def __init__(self, at, refs):
        self.at = at
        (
            self.pack, self.from_core, self.half, self.from_plane, self.line, self.fin,
            self.core_sem, self.plane_send, self.plane_recv, self.line_send, self.line_recv,
            self.back_send, self.back_recv, self.pass_send, self.pass_recv,
        ) = refs

    def put(self, index, value):
        for j in range(2):
            self.pack[pl.ds((2 * index + j) * 256, 256), :] = value[
                :, j * LANES : (j + 1) * LANES
            ].astype(BF16)

    def to_core(self):
        other_half = pl.multiple_of((1 - self.at.core) * 1024, 1024)
        self.first = send(
            self.pack.at[pl.ds(other_half, 1024)],
            self.from_core,
            self.core_sem.at[0],
            self.core_sem.at[1],
            self.at.other,
        )

    def to_plane(self):
        at = self.at
        self.first.wait()
        own_half = pl.multiple_of(at.core * 1024, 1024)
        self.half[...] = (
            self.pack[pl.ds(own_half, 1024), :].astype(F32) + self.from_core[...].astype(F32)
        ).astype(BF16)
        self.copies = []
        for k, (dy, dx) in enumerate(at.plane_steps):
            to = ((at.y + dy) % 4) * 4 + (at.x + dx) % 4
            self.copies.append(
                send(
                    self.half.at[pl.ds(pl.multiple_of(to * 64, 64), 64)],
                    self.from_plane.at[k],
                    self.plane_send.at[k],
                    self.plane_recv.at[k],
                    at.plane_ids[k],
                )
            )

    def to_line(self):
        at = self.at
        mine = pl.multiple_of((at.y * 4 + at.x) * 64, 64)
        total = self.half[pl.ds(mine, 64), :].astype(F32)
        for k, copy in enumerate(self.copies):
            copy.wait_recv()
            total = total + self.from_plane[k].astype(F32)
        self.line[at.z] = total.astype(BF16)
        self.lines = [
            send(
                self.line.at[at.z],
                self.line.at[at.z],
                self.line_send.at[k],
                self.line_recv.at[k],
                at.line_ids[k],
            )
            for k in range(7)
        ]

    def back(self):
        at = self.at
        for copy in self.lines:
            copy.wait_recv()
        total = self.line[0].astype(F32)
        for k in range(1, 8):
            total = total + self.line[k].astype(F32)
        mine = pl.multiple_of(at.core * 1024 + (at.y * 4 + at.x) * 64, 64)
        rows = self.fin.at[pl.ds(mine, 64)]
        self.fin[pl.ds(mine, 64), :] = total.astype(BF16)
        self.backs = [
            send(rows, rows, self.back_send.at[k], self.back_recv.at[k], at.plane_ids[k])
            for k in range(15)
        ]
        self.passes = [
            send(rows, rows, self.pass_send.at[15], self.pass_recv.at[15], at.other)
        ]

    def finish(self):
        at = self.at
        for k, (dy, dx) in enumerate(at.plane_steps):
            self.backs[k].wait_recv()
            came = ((at.y + 4 - dy) % 4) * 4 + (at.x + 4 - dx) % 4
            first = pl.multiple_of(at.core * 1024 + came * 64, 64)
            rows = self.fin.at[pl.ds(first, 64)]
            self.passes.append(
                send(rows, rows, self.pass_send.at[k], self.pass_recv.at[k], at.other)
            )
        for copy in self.passes:
            copy.wait()
        for copy in [*self.copies, *self.lines, *self.backs]:
            copy.wait_send()


def block_kernel(
    sig, cot, wq, wk, wv, wo, sq, sk, sv, so, nbr, val,
    bo_out, sg_out, fin_out,
    se, qe, ke, ve, me, lse, bias, pst, awb, mix_acc,
    rows_st, grads_st, cm, cb, qg, kg, vg, gg, acc_m, acc_q, acc_k, acc_v, flat,
    dq_b, dk_b, dv_b, mix_b, gr_st, bo_st, bo,
    gae, gme, delta, dq_acc, dk_acc, dv_acc,
    h_send, h_recv, a_send, a_recv, d_send, d_recv,
    *sum_refs,
):
    at = Place()
    barrier = pltpu.get_barrier_semaphore()
    known = [*at.stn_ids, at.left, at.right, *at.rim_sources, *at.plane_ids, *at.line_ids]
    for peer in known:
        pl.semaphore_signal(barrier, inc=1, device_id=peer, device_id_type=MESH)
    pl.semaphore_wait(barrier, len(known))
    station_sum = Sum(at, sum_refs[:15])
    window_sum = Sum(at, sum_refs[15:])

    def exchange(lane, source, target):
        return [
            send(
                source((at.stn + r) % STN),
                target(at.stn),
                a_send.at[lane, r - 1],
                a_recv.at[lane, r - 1],
                at.stn_ids[r - 1],
            )
            for r in range(1, STN)
        ]

    def sixteen(index):
        return pl.ds(pl.multiple_of(index * 16, 16), 16)

    halos = [
        send(sig.at[:, pl.ds(0, 128)], se.at[:, pl.ds(384, 128)], h_send.at[0], h_recv.at[0], at.left),
        send(sig.at[:, pl.ds(128, 128)], se.at[:, pl.ds(0, 128)], h_send.at[1], h_recv.at[1], at.right),
    ]
    to_frames = exchange(
        0, lambda d: cot.at[:, sixteen(d)], lambda m: grads_st.at[pl.ds(m * 2, 2)]
    )
    grads_st[pl.ds(at.stn * 2, 2)] = cot[:, sixteen(at.stn), :]

    scale = 0.125

    def project(s, first, rows):
        where = pl.ds(first, rows.shape[0])
        qe[s, where, :] = (dot(rows, wq[...]).astype(BF16) * scale).astype(BF16)
        ke[s, where, :] = dot(rows, wk[...]).astype(BF16)
        ve[s, where, :] = dot(rows, wv[...]).astype(BF16)

    for s in range(2):
        project(s, 128, sig[s])
    key = lax.broadcasted_iota(jnp.int32, (512, 256), 0)
    query = lax.broadcasted_iota(jnp.int32, (512, 256), 1)
    frame = key + (at.tm * 256 - HALF)
    seen = (key - query >= 0) & (key - query <= 2 * HALF) & (frame >= 0) & (frame < TM * 256)
    bias[...] = jnp.where(seen, 0.0, -1e30)
    target = lax.broadcasted_iota(jnp.int32, (32, 32), 1)
    counts = jnp.where(lax.broadcasted_iota(jnp.int32, (32, 32), 0) == target, 1.0, 0.0)
    for j in range(16):
        hit = (nbr[:, j : j + 1] == target) & (val[:, j : j + 1] == 1)
        counts = counts + jnp.where(hit, 1.0, 0.0)
    spread = jnp.where(
        lax.broadcasted_iota(jnp.int32, (256, 32), 0) // 8
        == lax.broadcasted_iota(jnp.int32, (256, 32), 1),
        1.0,
        0.0,
    ).astype(BF16)
    wide = dot(spread, dot(spread, counts.astype(BF16)).astype(BF16), "nt")
    same = (
        lax.broadcasted_iota(jnp.int32, (256, 256), 0) % 8
        == lax.broadcasted_iota(jnp.int32, (256, 256), 1) % 8
    )
    wide = jnp.where(same, wide, 0.0)
    cm[...] = wide
    cb[...] = jnp.where(wide > 0.0, 0.0, -1e30)

    lane_head = lax.broadcasted_iota(jnp.int32, (1, 256), 1) // 64

    def of_head(h):
        return jnp.where(lane_head == h, 1.0, 0.0).astype(BF16)

    for copy in halos:
        copy.wait_recv()
    for s in range(2):
        project(s, 0, se[s, 0:128, :])
        project(s, 384, se[s, 384:512, :])

    mix_acc[...] = jnp.zeros_like(mix_acc)

    def window_forward(i, carry):
        s, h = i // HEADS, i % HEADS
        mine = of_head(h)
        scores = dot(ke[s], qe[s, 128:384, :] * mine, "nt") + bias[...]
        highest = jnp.max(scores, axis=0, keepdims=True)
        raised = jnp.exp(scores - highest)
        total = jnp.sum(raised, axis=0, keepdims=True)
        probs = raised * (1.0 / total)
        pst[i] = probs
        lse[i, :, 128:384] = highest + jnp.log(total)
        mix_acc[s] += dot(probs.astype(BF16), ve[s] * mine, "tn")
        return carry

    lax.fori_loop(0, 2 * HEADS, window_forward, 0)
    for s in range(2):
        mixed = mix_acc[s].astype(BF16)
        me[s, 128:384, :] = mixed
        awb[s] = (sig[s].astype(F32) + dot(mixed, wo[...])).astype(BF16)
    to_rows = exchange(
        1, lambda d: awb.at[:, sixteen(d)], lambda m: rows_st.at[pl.ds(m * 2, 2)]
    )
    rows_st[pl.ds(at.stn * 2, 2)] = awb[:, sixteen(at.stn), :]
    rims = [
        send(me.at[:, pl.ds(128, 128)], me.at[:, pl.ds(384, 128)], h_send.at[2], h_recv.at[2], at.left),
        send(me.at[:, pl.ds(256, 128)], me.at[:, pl.ds(0, 128)], h_send.at[3], h_recv.at[3], at.right),
        send(lse.at[:, :, pl.ds(128, 128)], lse.at[:, :, pl.ds(384, 128)], h_send.at[4], h_recv.at[4], at.left),
        send(lse.at[:, :, pl.ds(256, 128)], lse.at[:, :, pl.ds(0, 128)], h_send.at[5], h_recv.at[5], at.right),
    ]

    def grouped(target_ref, value):
        parts = value.reshape(32, 2, 8, 256)
        for g in range(2):
            target_ref[g] = parts[:, g].reshape(256, 256).astype(BF16)

    for copy in to_frames:
        copy.wait_recv()
    grads = grads_st[...].reshape(512, 256)
    grouped(gg, dot(grads, so[...], "nt"))
    for ref in (acc_m, acc_q, acc_k, acc_v):
        ref[...] = jnp.zeros_like(ref)
    for copy in to_rows:
        copy.wait_recv()
    rows = rows_st[...].reshape(512, 256)
    grouped(qg, dot(rows, sq[...]).astype(BF16).astype(F32) * scale)
    grouped(kg, dot(rows, sk[...]))
    grouped(vg, dot(rows, sv[...]))

    def station(i, carry):
        g, h = i // HEADS, i % HEADS
        mine = of_head(h)
        q, k, v, gm = qg[g] * mine, kg[g] * mine, vg[g] * mine, gg[g] * mine
        scores = dot(k, q, "nt") + cb[...]
        highest = jnp.max(scores, axis=0, keepdims=True)
        raised = cm[...] * jnp.exp(scores - highest)
        probs = raised * (1.0 / jnp.sum(raised, axis=0, keepdims=True))
        weights = probs.astype(BF16)
        acc_m[g] += dot(weights, v, "tn")
        d_probs = dot(v, gm, "nt")
        moved = probs * d_probs
        d_scores = (moved - probs * jnp.sum(moved, axis=0, keepdims=True)).astype(BF16)
        acc_v[g] += dot(weights, gm)
        acc_q[g] += dot(d_scores, k, "tn")
        acc_k[g] += dot(d_scores, q)
        return carry

    lax.fori_loop(0, 2 * HEADS, station, 0)

    def ungroup(target_ref, acc, factor):
        for g in range(2):
            flat[:, g * 8 : (g + 1) * 8, :] = acc[g].reshape(32, 8, 256)
        value = flat[...].reshape(512, 256)
        if factor is not None:
            value = value * factor
        target_ref[...] = value.astype(BF16)

    ungroup(dq_b, acc_q, scale)
    ungroup(dk_b, acc_k, None)
    ungroup(dv_b, acc_v, None)
    ungroup(mix_b, acc_m, None)
    back_rows = (
        grads.astype(F32)
        + dot(dq_b[...], sq[...], "nt")
        + dot(dk_b[...], sk[...], "nt")
        + dot(dv_b[...], sv[...], "nt")
    )
    gr_st[...] = back_rows.astype(BF16).reshape(32, 16, 256)
    to_owner = exchange(
        2,
        lambda d: gr_st.at[pl.ds(d * 2, 2)],
        lambda m: gae.at[:, pl.ds(pl.multiple_of(128 + m * 16, 16), 16)],
    )
    rim_rows = pl.ds(pl.multiple_of((384 + at.stn * 16) % 512, 16), 16)
    to_rims = [
        send(
            gr_st.at[pl.ds((at.stn + r) % STN * 2, 2)],
            gae.at[:, rim_rows],
            d_send.at[r],
            d_recv.at[r],
            at.rim_ids[r],
        )
        for r in range(STN)
    ]
    gae[:, pl.ds(pl.multiple_of(128 + at.stn * 16, 16), 16), :] = gr_st[pl.ds(at.stn * 2, 2)]
    output = rows.astype(F32) + dot(mix_b[...], so[...])
    bo_st[...] = output.astype(BF16).reshape(32, 16, 256)
    to_output = exchange(
        3, lambda d: bo_st.at[pl.ds(d * 2, 2)], lambda m: bo.at[:, sixteen(m)]
    )
    bo[:, sixteen(at.stn), :] = bo_st[pl.ds(at.stn * 2, 2)]
    station_sum.put(0, dot(rows, dq_b[...], "tn"))
    station_sum.put(1, dot(rows, dk_b[...], "tn"))
    station_sum.put(2, dot(rows, dv_b[...], "tn"))
    station_sum.put(3, dot(mix_b[...], grads, "tn"))
    station_sum.to_core()

    for copy in rims:
        copy.wait_recv()
    for copy in [*to_owner, *to_rims]:
        copy.wait_recv()
    station_sum.to_plane()
    heads8 = jnp.where(
        lax.broadcasted_iota(jnp.int32, (8, 256), 1) // 64
        == lax.broadcasted_iota(jnp.int32, (8, 256), 0),
        1.0,
        0.0,
    ).astype(BF16)
    for s in range(2):
        gmix = dot(gae[s], wo[...], "nt").astype(BF16)
        gme[s] = gmix
        product = gmix.astype(F32) * me[s].astype(F32)
        high = product.astype(BF16)
        low = (product - high.astype(F32)).astype(BF16)
        sums = dot(heads8, high, "nt") + dot(heads8, low, "nt")
        for h in range(HEADS):
            delta[s * HEADS + h] = sums[h : h + 1, :]
    window_sum.put(
        3,
        dot(
            me[:, 128:384, :].reshape(512, 256), gae[:, 128:384, :].reshape(512, 256), "tn"
        ),
    )
    for ref in (dq_acc, dk_acc, dv_acc):
        ref[...] = jnp.zeros_like(ref)
    rim_key = lax.broadcasted_iota(jnp.int32, (128, 128), 0)
    rim_query = lax.broadcasted_iota(jnp.int32, (128, 128), 1)

    def window_backward(i, carry):
        s, h = i // HEADS, i % HEADS
        mine = of_head(h)
        q, k, g = qe[s] * mine, ke[s] * mine, gme[s] * mine
        v = ve[s]
        probs = pst[i]
        d_scores = (
            probs * (dot(v, g[128:384], "nt") - delta[i, :, 128:384])
        ).astype(BF16)
        weights = probs[128:384].astype(BF16)
        dq_acc[s] += dot(d_scores, k, "tn")
        d_key = dot(d_scores[128:384], q[128:384])
        d_value = dot(weights, g[128:384])

        def rim(keys, queries, allowed):
            scores = dot(k[keys : keys + 128], q[queries : queries + 128], "nt")
            scores = jnp.where(allowed, scores - lse[i, :, queries : queries + 128], -1e30)
            rim_probs = jnp.exp(scores)
            g_rim = g[queries : queries + 128]
            rim_scores = rim_probs * (
                dot(v[keys : keys + 128], g_rim, "nt") - delta[i, :, queries : queries + 128]
            )
            return (
                dot(rim_scores.astype(BF16), q[queries : queries + 128]),
                dot(rim_probs.astype(BF16), g_rim),
            )

        left_key, left_value = rim(128, 0, (rim_key <= rim_query) & (at.tm > 0))
        right_key, right_value = rim(256, 384, (rim_query <= rim_key) & (at.tm < TM - 1))
        dk_acc[s, 0:128, :] += d_key[0:128] + left_key
        dk_acc[s, 128:256, :] += d_key[128:256] + right_key
        dv_acc[s, 0:128, :] += d_value[0:128] + left_value
        dv_acc[s, 128:256, :] += d_value[128:256] + right_value
        return carry

    lax.fori_loop(0, 2 * HEADS, window_backward, 0)
    station_sum.to_line()
    signal = sig[...].reshape(512, 256)
    d_query = (dq_acc[...].reshape(512, 256) * scale).astype(BF16)
    d_key = dk_acc[...].reshape(512, 256).astype(BF16)
    d_value = dv_acc[...].reshape(512, 256).astype(BF16)
    window_sum.put(0, dot(signal, d_query, "tn"))
    window_sum.put(1, dot(signal, d_key, "tn"))
    window_sum.put(2, dot(signal, d_value, "tn"))
    window_sum.to_core()
    signal_grad = (
        gae[:, 128:384, :].reshape(512, 256).astype(F32)
        + dot(d_query, wq[...], "nt")
        + dot(d_key, wk[...], "nt")
        + dot(d_value, wv[...], "nt")
    )
    sg_out[...] = signal_grad.astype(BF16).reshape(2, 256, 256)
    window_sum.to_plane()
    station_sum.back()
    window_sum.to_line()
    window_sum.back()
    station_sum.finish()
    for copy in to_output:
        copy.wait_recv()
    bo_out[...] = bo[...]
    window_sum.finish()
    for copy in [*halos, *to_frames, *to_rows, *rims, *to_owner, *to_rims, *to_output]:
        copy.wait_send()
    fin_out[0:2048, :] = window_sum.fin[...]
    fin_out[2048:4096, :] = station_sum.fin[...]


def sum_scratch():
    dma = pltpu.SemaphoreType.DMA
    return [
        pltpu.VMEM((2048, LANES), BF16),
        pltpu.VMEM((1024, LANES), BF16),
        pltpu.VMEM((1024, LANES), BF16),
        pltpu.VMEM((15, 64, LANES), BF16),
        pltpu.VMEM((8, 64, LANES), BF16),
        pltpu.VMEM((2048, LANES), BF16),
        dma((2,)), dma((15,)), dma((15,)), dma((7,)), dma((7,)),
        dma((15,)), dma((15,)), dma((16,)), dma((16,)),
    ]


def finish_kernel(factor, bo, sg, fin, o_bo, o_sg, o_wq, o_wk, o_wv, o_wo, o_sq, o_sk, o_sv, o_so):
    o_bo[...] = bo[...]
    o_sg[...] = sg[...]
    for i, ref in enumerate((o_wq, o_wk, o_wv, o_wo, o_sq, o_sk, o_sv, o_so)):
        for j in range(2):
            ref[:, j * LANES : (j + 1) * LANES] = (
                fin[pl.ds((2 * i + j) * 256, 256), :].astype(F32) * factor
            )


def body(signal, cotangent, *rest):
    dma = pltpu.SemaphoreType.DMA
    vmem = pl.BlockSpec(memory_space=pltpu.VMEM)

    def b(*shape):
        return pltpu.VMEM(shape, BF16)

    def f(*shape):
        return pltpu.VMEM(shape, F32)

    scratch = [
        b(2, 512, 256), b(2, 512, 256), b(2, 512, 256), b(2, 512, 256), b(2, 512, 256),
        f(8, 1, 512), f(512, 256), f(8, 512, 256), b(2, 256, 256), f(2, 256, 256),
        b(32, 16, 256), b(32, 16, 256), f(256, 256), f(256, 256),
        b(2, 256, 256), b(2, 256, 256), b(2, 256, 256), b(2, 256, 256),
        f(2, 256, 256), f(2, 256, 256), f(2, 256, 256), f(2, 256, 256), f(32, 16, 256),
        b(512, 256), b(512, 256), b(512, 256), b(512, 256),
        b(32, 16, 256), b(32, 16, 256), b(2, 256, 256),
        b(2, 512, 256), b(2, 512, 256), f(8, 1, 512),
        f(2, 256, 256), f(2, 256, 256), f(2, 256, 256),
        dma((6,)), dma((6,)), dma((4, 15)), dma((4, 15)), dma((16,)), dma((16,)),
        *sum_scratch(), *sum_scratch(),
    ]
    block_output, signal_grad, fin = pl.pallas_call(
        block_kernel,
        out_shape=[
            jax.ShapeDtypeStruct((2, 256, 256), BF16),
            jax.ShapeDtypeStruct((2, 256, 256), BF16),
            jax.ShapeDtypeStruct((4096, LANES), BF16),
        ],
        in_specs=[vmem] * 12,
        out_specs=[vmem] * 3,
        scratch_shapes=scratch,
        compiler_params=pltpu.CompilerParams(
            collective_id=0, has_side_effects=True, vmem_limit_bytes=48 * 1024 * 1024
        ),
        name="block",
    )(signal, cotangent, *rest)
    factor = 1.0 / math.sqrt(STN * 2 * TM * 256)
    return pl.pallas_call(
        functools.partial(finish_kernel, factor),
        out_shape=[
            jax.ShapeDtypeStruct((2, 256, 256), BF16),
            jax.ShapeDtypeStruct((2, 256, 256), BF16),
        ]
        + [jax.ShapeDtypeStruct((256, 256), F32)] * 8,
        in_specs=[vmem] * 3,
        out_specs=[vmem] * 10,
        name="finish",
    )(block_output, signal_grad, fin)


def solution(mesh):
    return jax.shard_map(
        lambda *operands: tuple(body(*operands)),
        mesh=mesh,
        in_specs=(P("stn", "tm", None), P("stn", "tm", None), *([P()] * 10)),
        out_specs=(P("stn", "tm", None), P("stn", "tm", None), *([P()] * 8)),
        check_vma=False,
    )
```

time: 434 us -> 102 us (0.24)
  waiting for transfers between devices: 287 us -> 0 us
  Pallas kernels: 0 us -> 88.1 us
  matrix products: 40.2 us -> 0 us
  starting transfers between devices: 30.1 us -> 0 us
  local copies, waits for them, and re-layouts: 34.3 us -> 12.4 us
  blocking collectives: 15 us -> 0 us
  between operations: 14.8 us -> 0.68 us
  other arithmetic: 11.1 us -> 0 us
    psum x1 -> x0, waiting for transfers between devices: 253 us -> none  [body(): lax.psum((grad_wq, grad_wkv, grad_wo, grad_sqkv, grad_so), ('stn', 'tm'))]
    pallas_call x0 -> x2, Pallas kernels: none -> 88.1 us  [the longest x1 85.2 us: body(): pl.pallas_call(block_kernel, out_shape=[jax.ShapeDtypeStruct((2, 256, 256...]
    dot_general x31 -> x0, matrix products: 34.3 us -> none  [the longest x2 5.76 us: window_backward(): jnp.einsum('hqk,qhd->khd', weights, split_g, preferred_element_type=jnp.f...]
    all_to_all x3 -> x0, starting transfers between devices: 21.4 us -> none  [the longest x1 8.73 us: body(): lax.all_to_all(after_window, 'stn', split_axis=1, concat_axis=0, tiled=True)]
    ppermute x4 -> x0, waiting for transfers between devices: 19.7 us -> none  [the longest x2 15.5 us: with_halo(): lax.ppermute(head, axis, [((i + 1) % count, i) for i in range(ends)])]
    all_to_all x1 -> x0, blocking collectives: 15 us -> none  [body(): lax.all_to_all(station_output, 'stn', split_axis=0, concat_axis=1, tiled=...]
    all_to_all x3 -> x0, waiting for transfers between devices: 14 us -> none  [the longest x1 7.41 us: body(): lax.all_to_all(station_back, 'stn', split_axis=0, concat_axis=1, tiled=True)]
    ppermute x4 -> x0, starting transfers between devices: 8.69 us -> none  [the longest x2 6.1 us: with_halo(): lax.ppermute(tail, axis, [(i, (i + 1) % count) for i in range(ends)])]
  transfers between devices with their start and end apart: 8 -> 0, of which waited for: 7 -> 0; matrix products, arithmetic and copies ran while one was open for 6% -> 0% of each run, Pallas kernels for 0% -> 0%
where the time goes in v2:
time: 102 us; the launch traced here: 101 us
  Pallas kernels  88.1 us (86%)
  local copies, waits for them, and re-layouts  12.4 us (12%)
    pallas_call x1, Pallas kernels, body(): pl.pallas_call(block_kernel, out_shape=[jax.ShapeDtypeStruct((2, 256, 256...  85.2 us
    unnamed x30, local copies, waits for them, and re-layouts  12.4 us
    pallas_call x1, Pallas kernels, body(): pl.pallas_call(functools.partial(finish_kernel, factor), out_shape=[jax.S...  2.89 us

profile of v2, /device:TPU:1, one launch (start us, length us, event | category | flops | bytes accessed | tf_op | source)
XLA Modules:
  0.0 101.2 jit_solution(15110041463967646921)
XLA Ops:
  0.6 0.0 copy-start.13
  0.7 0.8 copy.22.nbr
  1.4 0.0 copy-done.13
  1.4 0.1 copy.23.val
  1.5 0.0 copy-start.1
  1.5 1.0 copy-done.1
  2.5 0.0 copy-start.2
  2.5 0.9 copy-done.2
  3.4 0.0 copy-start.5
  3.4 0.9 copy-done.5
  4.3 0.0 copy-start.6
  4.3 0.9 copy-done.6
  5.2 0.0 copy-start.7
  5.2 0.9 copy-done.7
  6.1 0.0 copy-start.8
  6.1 0.9 copy-done.8
  7.0 0.0 copy-start.9
  7.0 0.9 copy-done.9
  7.9 0.0 copy-start.10
  7.9 0.9 copy-done.10
  8.8 0.0 copy-start.11
  8.8 0.9 copy-done.11
  9.7 0.0 copy-start.12
  9.7 0.9 copy-done.12
  10.6 85.2 %block.1 = (bf16[2,256,256]{2,1,0:T(8,128)(2,1)S(1)}, bf16[2,256,256]{2,1,0:T(8,128)(2,1)S(1)}, bf16[4096,128]{1,0:T(8,128)(2,1)S(1)}) custom-call(bf16[2,256,256]{2,1,0:T(8,128)(2,1)S(1)} %copy-done.1, bf16[2,256,256]{2,1,0:T(8,128)(2,1)S(1)} %copy-done.2, bf16[256,256]{1,0:T(8,128)(2,1)S(1)} %copy-done.5, bf16[256,256]{1,0:T(8,128)(2,1)S(1)} %copy-done.6, ...), custom_call_target="tpu_custom_call" | custom-call | tf_op jit(solution)/shard_map/block/pallas_call | solution.py:518
  95.9 0.0 copy-start
  95.9 1.0 copy-done
  96.9 0.0 copy-start.3
  96.9 0.7 copy-done.3
  97.6 0.0 copy-start.4
  97.6 0.7 copy-done.4
  98.3 2.9 %finish.1 = (bf16[2,256,256]{2,1,0:T(8,128)(2,1)}, bf16[2,256,256]{2,1,0:T(8,128)(2,1)}, f32[256,256]{1,0:T(8,128)}, f32[256,256]{1,0:T(8,128)}, f32[256,256]{1,...) custom-call(bf16[2,256,256]{2,1,0:T(8,128)(2,1)} %copy-done.3, ...), custom_call_target="tpu_custom_call" | custom-call | tf_op jit(solution)/shard_map/finish/pallas_call | solution.py:534
Async XLA Ops:
  0.6 0.8 copy-start.13
  1.5 1.0 copy-start.1
  2.5 0.9 copy-start.2
  3.4 0.9 copy-start.5
  4.3 0.9 copy-start.6
  5.2 0.9 copy-start.7
  6.1 0.9 copy-start.8
  7.0 0.9 copy-start.9
  7.9 0.9 copy-start.10
  8.8 0.9 copy-start.11
  9.7 0.9 copy-start.12
  95.9 1.0 copy-start
  96.9 0.7 copy-start.3
  97.6 0.7 copy-start.4

commit v3 on v2

v3 whole, which is shorter than its diff:
```python
import functools
import math

import jax
import jax.numpy as jnp
from jax import lax
from jax.experimental import pallas as pl
from jax.experimental.pallas import tpu as pltpu
from jax.sharding import PartitionSpec as P

HEADS = 4
HALF = 128
LANES = 128
MESH = pl.DeviceIdType.MESH
F32 = jnp.float32
BF16 = jnp.bfloat16
STN = 16
TM = 16


def rem(a, n):
    return lax.rem(a, jnp.int32(n))


def div(a, n):
    return lax.div(a, jnp.int32(n))


def dot(a, b, kind="nn"):
    dims = {"nn": ((1,), (0,)), "nt": ((1,), (1,)), "tn": ((0,), (0,))}[kind]
    return lax.dot_general(a, b, (dims, ((), ())), preferred_element_type=F32)


def device_at(y, x, z, core):
    return ((y * 2 + div(x, 2)) * 2 + core, z * 2 + rem(x, 2))


def send(src, dst, send_sem, recv_sem, peer):
    copy = pltpu.make_async_remote_copy(
        src_ref=src,
        dst_ref=dst,
        send_sem=send_sem,
        recv_sem=recv_sem,
        device_id=peer,
        device_id_type=MESH,
    )
    copy.start()
    return copy


class Place:
    def __init__(self):
        self.stn = lax.axis_index("stn")
        self.tm = lax.axis_index("tm")
        self.core = rem(self.stn, 2)
        self.x = rem(div(self.stn, 2), 2) * 2 + rem(self.tm, 2)
        self.y = div(self.stn, 4)
        self.z = div(self.tm, 2)
        y, x, z, core = self.y, self.x, self.z, self.core
        self.other = device_at(y, x, z, 1 - core)
        self.plane_steps = [(dy, dx) for dy in range(4) for dx in range(4) if dy + dx > 0]
        ys = [rem(y + d, 4) for d in range(4)]
        xs = [rem(x + d, 4) for d in range(4)]
        zs = [rem(z + d, 8) for d in range(8)]
        self.plane_to = [ys[dy] * 4 + xs[dx] for dy, dx in self.plane_steps]
        self.plane_from = [ys[-dy % 4] * 4 + xs[-dx % 4] for dy, dx in self.plane_steps]
        self.plane_ids = [device_at(ys[dy], xs[dx], z, core) for dy, dx in self.plane_steps]
        self.line_ids = [device_at(y, x, zs[d], core) for d in range(1, 8)]
        self.stns = [rem(self.stn + r, STN) for r in range(STN)]
        self.stn_ids = [(self.stns[r], self.tm) for r in range(1, STN)]
        self.left = (self.stn, rem(self.tm + TM - 1, TM))
        self.right = (self.stn, rem(self.tm + 1, TM))
        beside = rem(self.tm + TM - 1 + 2 * div(self.stn, 8), TM)
        self.rim_ids = [(self.stns[r], beside) for r in range(STN)]
        self.rim_sources = []
        for r in range(STN):
            source = self.stns[-r % STN]
            self.rim_sources.append((source, rem(self.tm + TM + 1 - 2 * div(source, 8), TM)))


class Sum:
    def __init__(self, at, count, refs):
        self.at = at
        self.rows = count * 16
        self.half_rows = count * 256
        (
            self.pack, self.from_core, self.half, self.from_plane, self.line, self.fin,
            self.core_sem, self.plane_send, self.plane_recv, self.line_send, self.line_recv,
            self.back_send, self.back_recv, self.pass_send, self.pass_recv,
        ) = refs

    def put(self, index, value):
        for j in range(2):
            self.pack[pl.ds((2 * index + j) * 256, 256), :] = value[
                :, j * LANES : (j + 1) * LANES
            ].astype(BF16)

    def slot(self, index):
        return pl.ds(pl.multiple_of(index * self.rows, self.rows), self.rows)

    def final(self, index):
        first = self.at.core * self.half_rows + index * self.rows
        return pl.ds(pl.multiple_of(first, self.rows), self.rows)

    def to_core(self):
        other_half = pl.multiple_of((1 - self.at.core) * self.half_rows, self.half_rows)
        self.first = send(
            self.pack.at[pl.ds(other_half, self.half_rows)],
            self.from_core,
            self.core_sem.at[0],
            self.core_sem.at[1],
            self.at.other,
        )

    def to_plane(self):
        at = self.at
        self.first.wait()
        own_half = pl.multiple_of(at.core * self.half_rows, self.half_rows)
        self.half[...] = (
            self.pack[pl.ds(own_half, self.half_rows), :].astype(F32)
            + self.from_core[...].astype(F32)
        ).astype(BF16)
        self.copies = [
            send(
                self.half.at[self.slot(at.plane_to[k])],
                self.from_plane.at[k],
                self.plane_send.at[k],
                self.plane_recv.at[k],
                at.plane_ids[k],
            )
            for k in range(15)
        ]

    def to_line(self):
        at = self.at
        total = self.half[self.slot(at.y * 4 + at.x), :].astype(F32)
        for k, copy in enumerate(self.copies):
            copy.wait_recv()
            total = total + self.from_plane[k].astype(F32)
        self.line[at.z] = total.astype(BF16)
        self.lines = [
            send(
                self.line.at[at.z],
                self.line.at[at.z],
                self.line_send.at[k],
                self.line_recv.at[k],
                at.line_ids[k],
            )
            for k in range(7)
        ]

    def back(self):
        at = self.at
        for copy in self.lines:
            copy.wait_recv()
        total = self.line[0].astype(F32)
        for k in range(1, 8):
            total = total + self.line[k].astype(F32)
        mine = self.final(at.y * 4 + at.x)
        rows = self.fin.at[mine]
        self.fin[mine, :] = total.astype(BF16)
        self.backs = [
            send(rows, rows, self.back_send.at[k], self.back_recv.at[k], at.plane_ids[k])
            for k in range(15)
        ]
        self.passes = [
            send(rows, rows, self.pass_send.at[15], self.pass_recv.at[15], at.other)
        ]

    def pass_on(self):
        at = self.at
        for k in range(15):
            self.backs[k].wait_recv()
            rows = self.fin.at[self.final(at.plane_from[k])]
            self.passes.append(
                send(rows, rows, self.pass_send.at[k], self.pass_recv.at[k], at.other)
            )

    def finish(self):
        for copy in self.passes:
            copy.wait()
        for copy in [*self.copies, *self.lines, *self.backs]:
            copy.wait_send()


def iota(shape, dim):
    return lax.broadcasted_iota(jnp.int32, shape, dim)


def four(value):
    return jnp.concatenate([value] * HEADS, axis=1)


def stack(rows):
    head = iota((1, 256), 1) // 64
    return jnp.concatenate(
        [rows * jnp.where(head == h, 1.0, 0.0).astype(BF16) for h in range(HEADS)], axis=0
    )


def by_rows(tile):
    return jnp.concatenate([tile[:, h * 128 : (h + 1) * 128] for h in range(HEADS)], axis=0)


def block_kernel(
    sig_in, cot, wq_in, wk_in, wv_in, wo_in, sq_in, sk_in, sv_in, so_in, nbr_in, val_in,
    bo_out, sg_out, fin_out,
    sig, weights, nbr, val,
    se, qe, ke, ve, me, lse, bias_own, bias_halo, bias_rim, own_top, own_sum,
    probs_own, probs_halo, probs_rim, awb,
    rows_st, grads_st, cm, cb, perm, perm_back, qg, kg, vg, gg,
    dq_b, dk_b, dv_b, mix_b, gr_st, bo_st, bo,
    gae, gme, delta, dq_w,
    in_sem, h_send, h_recv, a_send, a_recv, d_send, d_recv,
    *sum_refs,
):
    wq, wk, wv, wo, sq, sk, sv, so = (weights.at[i] for i in range(8))
    fetches = [pltpu.make_async_copy(sig_in, sig, in_sem.at[0])]
    for i, ref in enumerate((wq_in, wk_in, wv_in, wo_in, sq_in, sk_in, sv_in, so_in)):
        fetches.append(pltpu.make_async_copy(ref, weights.at[i], in_sem.at[1 + i]))
    fetches.append(pltpu.make_async_copy(nbr_in, nbr, in_sem.at[9]))
    fetches.append(pltpu.make_async_copy(val_in, val, in_sem.at[10]))
    for copy in fetches:
        copy.start()
    at = Place()
    barrier = pltpu.get_barrier_semaphore()
    known = [at.left, at.right, *at.stn_ids, *at.rim_sources, *at.plane_ids, *at.line_ids]
    for peer in known:
        pl.semaphore_signal(barrier, inc=1, device_id=peer, device_id_type=MESH)

    def sixteen(index, base=0):
        return pl.ds(pl.multiple_of(base + index * 16, 16), 16)

    own_cot = pltpu.make_async_copy(
        cot.at[:, sixteen(at.stn)], grads_st.at[pl.ds(at.stn * 2, 2)], in_sem.at[11]
    )
    own_cot.start()
    pl.semaphore_wait(barrier, len(known))
    station_sum = Sum(at, 5, sum_refs[:15])
    window_sum = Sum(at, 3, sum_refs[15:])

    def exchange(lane, source, target):
        return [
            send(
                source(at.stns[r]),
                target(at.stn),
                a_send.at[lane, r - 1],
                a_recv.at[lane, r - 1],
                at.stn_ids[r - 1],
            )
            for r in range(1, STN)
        ]

    def beside(lane, first, last, to_right, to_left):
        return [
            send(first, to_left, h_send.at[lane], h_recv.at[lane], at.left),
            send(last, to_right, h_send.at[lane + 1], h_recv.at[lane + 1], at.right),
        ]

    halos = beside(
        0,
        sig_in.at[:, pl.ds(0, 128)],
        sig_in.at[:, pl.ds(128, 128)],
        se.at[:, pl.ds(0, 128)],
        se.at[:, pl.ds(384, 128)],
    )
    for copy in fetches:
        copy.wait()
    scale = 0.125

    def project(s, first, rows):
        where = pl.ds(first, rows.shape[0])
        qe[s, where, :] = (dot(rows, wq[...]).astype(BF16) * scale).astype(BF16)
        ke[s, where, :] = dot(rows, wk[...]).astype(BF16)
        ve[s, where, :] = dot(rows, wv[...]).astype(BF16)

    for s in range(2):
        project(s, 128, sig[s])
    low = -1e30
    key = iota((256, 128), 0)
    query = iota((256, 128), 1)
    for half in range(2):
        offset = key - query - 128 * half
        bias_own[half] = four(jnp.where((offset <= HALF) & (offset >= -HALF), 0.0, low))
    key = iota((128, 128), 0)
    query = iota((128, 128), 1)
    has_left = at.tm > 0
    has_right = at.tm < TM - 1
    bias_halo[0] = four(jnp.where((key >= query) & has_left, 0.0, low))
    bias_halo[1] = four(jnp.where((key <= query) & has_right, 0.0, low))
    bias_rim[0] = four(jnp.where((key <= query) & has_left, 0.0, low))
    bias_rim[1] = four(jnp.where((key >= query) & has_right, 0.0, low))

    def own_scores(unit, carry):
        s, half = unit // 2, unit % 2
        queries = stack(qe[s, pl.ds(pl.multiple_of(128 + half * 128, 128), 128), :])
        scores = dot(ke[s, 128:384, :], queries, "nt") + bias_own[half]
        top = jnp.max(scores, axis=0, keepdims=True)
        raised = jnp.exp(scores - top)
        probs_own[unit] = raised
        own_top[unit] = top
        own_sum[unit] = jnp.sum(raised, axis=0, keepdims=True)
        return carry

    lax.fori_loop(0, 4, own_scores, 0)
    to_frames = exchange(
        0, lambda d: cot.at[:, sixteen(d)], lambda m: grads_st.at[pl.ds(m * 2, 2)]
    )
    target = iota((32, 32), 0)
    counts = jnp.where(iota((32, 32), 1) == target, 1.0, 0.0)
    for j in range(16):
        hit = (nbr[j : j + 1, :] == target) & (val[j : j + 1, :] == 1)
        counts = counts + jnp.where(hit, 1.0, 0.0)
    spread = jnp.where(iota((128, 32), 0) // 4 == iota((128, 32), 1), 1.0, 0.0).astype(BF16)
    wide = dot(dot(spread, counts.astype(BF16)).astype(BF16), spread, "nt")
    wide = jnp.where(iota((128, 128), 0) % 4 == iota((128, 128), 1) % 4, wide, 0.0)
    cm[...] = four(wide)
    cb[...] = four(jnp.where(wide > 0.0, 0.0, low))

    def placed(row):
        return row % 128 // 4 * 16 + row // 128 * 4 + row % 4

    perm[...] = jnp.where(placed(iota((512, 1), 0)) == iota((512, 512), 1), 1.0, 0.0).astype(BF16)
    perm_back[...] = jnp.where(
        placed(iota((1, 512), 1)) == iota((512, 512), 0), 1.0, 0.0
    ).astype(BF16)

    for copy in halos:
        copy.wait_recv()
    to_rows = []
    for s in range(2):
        project(s, 0, se[s, 0:128, :])
        project(s, 384, se[s, 384:512, :])
        for half in range(2):
            unit = 2 * s + half
            halo = 384 * half
            queries = stack(qe[s, 128 + half * 128 : 256 + half * 128, :])
            scores = dot(ke[s, halo : halo + 128, :], queries, "nt") + bias_halo[half]
            top = jnp.maximum(own_top[unit], jnp.max(scores, axis=0, keepdims=True))
            raised = jnp.exp(scores - top)
            shift = jnp.exp(own_top[unit] - top)
            total = own_sum[unit] * shift + jnp.sum(raised, axis=0, keepdims=True)
            lse[1 + half, s] = top + jnp.log(total)
            inverse = 1.0 / total
            p_own = probs_own[unit] * (shift * inverse)
            p_halo = raised * inverse
            probs_own[unit] = p_own
            probs_halo[unit] = p_halo
            mixed = (
                dot(by_rows(p_own.astype(BF16)), stack(ve[s, 128:384, :]), "tn")
                + dot(by_rows(p_halo.astype(BF16)), stack(ve[s, halo : halo + 128, :]), "tn")
            ).astype(BF16)
            me[s, 128 + half * 128 : 256 + half * 128, :] = mixed
        awb[s] = (sig[s].astype(F32) + dot(me[s, 128:384, :], wo[...])).astype(BF16)
        to_rows += exchange(
            1 + s, lambda d: awb.at[s, sixteen(d)], lambda m: rows_st.at[m * 2 + s]
        )
    rows_st[pl.ds(at.stn * 2, 2)] = awb[:, sixteen(at.stn), :]

    own_cot.wait()
    for copy in to_frames:
        copy.wait_recv()
    grads = dot(perm[...], grads_st[...].reshape(512, 256)).astype(BF16)
    gg[...] = dot(grads, so[...], "nt").astype(BF16)
    for copy in to_rows:
        copy.wait_recv()
    rims = [
        *beside(
            2,
            me.at[:, pl.ds(128, 128)],
            me.at[:, pl.ds(256, 128)],
            me.at[:, pl.ds(0, 128)],
            me.at[:, pl.ds(384, 128)],
        ),
        *beside(4, lse.at[1], lse.at[2], lse.at[0], lse.at[3]),
    ]
    rows = dot(perm[...], rows_st[...].reshape(512, 256)).astype(BF16)
    qg[...] = (dot(rows, sq[...]).astype(BF16) * scale).astype(BF16)
    kg[...] = dot(rows, sk[...]).astype(BF16)
    vg[...] = dot(rows, sv[...]).astype(BF16)

    def station(g, carry):
        part = pl.ds(pl.multiple_of(g * 128, 128), 128)
        k, v = kg[part, :], vg[part, :]
        q4, g4 = stack(qg[part, :]), stack(gg[part, :])
        scores = dot(k, q4, "nt") + cb[...]
        raised = cm[...] * jnp.exp(scores - jnp.max(scores, axis=0, keepdims=True))
        probs = raised * (1.0 / jnp.sum(raised, axis=0, keepdims=True))
        narrow = probs.astype(BF16)
        mix_b[part, :] = dot(by_rows(narrow), stack(v), "tn").astype(BF16)
        moved = probs * dot(v, g4, "nt")
        d_scores = (moved - probs * jnp.sum(moved, axis=0, keepdims=True)).astype(BF16)
        dv_b[part, :] = dot(narrow, g4).astype(BF16)
        dq_b[part, :] = (dot(by_rows(d_scores), stack(k), "tn") * scale).astype(BF16)
        dk_b[part, :] = dot(d_scores, q4).astype(BF16)
        return carry

    lax.fori_loop(0, 4, station, 0)
    back_rows = (
        grads.astype(F32)
        + dot(dq_b[...], sq[...], "nt")
        + dot(dk_b[...], sk[...], "nt")
        + dot(dv_b[...], sv[...], "nt")
    ).astype(BF16)
    gr_st[...] = dot(perm_back[...], back_rows).astype(BF16).reshape(32, 16, 256)
    to_owner = exchange(
        3, lambda d: gr_st.at[pl.ds(d * 2, 2)], lambda m: gae.at[:, sixteen(m, 128)]
    )
    rim_rows = pl.ds(pl.multiple_of(rem(384 + at.stn * 16, 512), 16), 16)
    to_rims = [
        send(
            gr_st.at[pl.ds(at.stns[r] * 2, 2)],
            gae.at[:, rim_rows],
            d_send.at[r],
            d_recv.at[r],
            at.rim_ids[r],
        )
        for r in range(STN)
    ]
    gae[:, sixteen(at.stn, 128), :] = gr_st[pl.ds(at.stn * 2, 2)]
    output = (rows.astype(F32) + dot(mix_b[...], so[...])).astype(BF16)
    bo_st[...] = dot(perm_back[...], output).astype(BF16).reshape(32, 16, 256)
    bo[:, sixteen(at.stn), :] = bo_st[pl.ds(at.stn * 2, 2)]
    station_sum.put(0, dot(rows, dq_b[...], "tn"))
    station_sum.put(1, dot(rows, dk_b[...], "tn"))
    station_sum.put(2, dot(rows, dv_b[...], "tn"))
    station_sum.put(3, dot(mix_b[...], grads, "tn"))

    for copy in rims:
        copy.wait_recv()

    def rim_scores(unit, carry):
        s, side = unit // 2, unit % 2
        queries = stack(qe[s, pl.ds(pl.multiple_of(384 * side, 128), 128), :])
        keys = ke[s, pl.ds(pl.multiple_of(128 + side * 128, 128), 128), :]
        scores = dot(keys, queries, "nt") + bias_rim[side]
        probs_rim[unit] = jnp.exp(scores - lse[3 * side, s])
        return carry

    lax.fori_loop(0, 4, rim_scores, 0)
    for copy in [*to_owner, *to_rims]:
        copy.wait_recv()
    to_output = exchange(
        4, lambda d: bo_st.at[pl.ds(d * 2, 2)], lambda m: bo.at[:, sixteen(m)]
    )
    heads8 = jnp.where(iota((8, 256), 1) // 64 == iota((8, 256), 0), 1.0, 0.0).astype(BF16)
    for s in range(2):
        gmix = dot(gae[s], wo[...], "nt").astype(BF16)
        gme[s] = gmix
        product = gmix.astype(F32) * me[s].astype(F32)
        high = product.astype(BF16)
        rest = (product - high.astype(F32)).astype(BF16)
        sums = dot(heads8, high, "nt") + dot(heads8, rest, "nt")
        for slot in range(4):
            for h in range(HEADS):
                delta[slot, s, :, h * 128 : (h + 1) * 128] = sums[
                    h : h + 1, slot * 128 : (slot + 1) * 128
                ]
    own_grads = gae[:, 128:384, :].reshape(512, 256)
    station_sum.put(4, dot(me[:, 128:384, :].reshape(512, 256), own_grads, "tn"))
    station_sum.to_core()

    for s in range(2):
        d_key = jnp.zeros((256, 256), F32)
        d_value = jnp.zeros((256, 256), F32)
        for half in range(2):
            unit = 2 * s + half
            halo = 384 * half
            first = 128 + half * 128
            g4 = stack(gme[s, first : first + 128, :])
            q4 = stack(qe[s, first : first + 128, :])
            p_own, p_halo = probs_own[unit], probs_halo[unit]
            drop = delta[1 + half, s]
            ds_own = (p_own * (dot(ve[s, 128:384, :], g4, "nt") - drop)).astype(BF16)
            ds_halo = (p_halo * (dot(ve[s, halo : halo + 128, :], g4, "nt") - drop)).astype(BF16)
            dq_w[s, half * 128 : half * 128 + 128, :] = (
                (
                    dot(by_rows(ds_own), stack(ke[s, 128:384, :]), "tn")
                    + dot(by_rows(ds_halo), stack(ke[s, halo : halo + 128, :]), "tn")
                )
                * scale
            ).astype(BF16)
            d_key = d_key + dot(ds_own, q4)
            d_value = d_value + dot(p_own.astype(BF16), g4)
        rim_key, rim_value = [], []
        for side in range(2):
            rim = 384 * side
            g4 = stack(gme[s, rim : rim + 128, :])
            q4 = stack(qe[s, rim : rim + 128, :])
            p_rim = probs_rim[2 * s + side]
            values = ve[s, 128 + side * 128 : 256 + side * 128, :]
            ds_rim = (p_rim * (dot(values, g4, "nt") - delta[3 * side, s])).astype(BF16)
            rim_key.append(dot(ds_rim, q4))
            rim_value.append(dot(p_rim.astype(BF16), g4))
        own = pl.ds(s * 256, 256)
        qg[own, :] = (d_key + jnp.concatenate(rim_key, axis=0)).astype(BF16)
        kg[own, :] = (d_value + jnp.concatenate(rim_value, axis=0)).astype(BF16)
        if s == 0:
            station_sum.to_plane()
    signal = sig[...].reshape(512, 256)
    d_query, d_key, d_value = dq_w[...].reshape(512, 256), qg[...], kg[...]
    window_sum.put(0, dot(signal, d_query, "tn"))
    window_sum.put(1, dot(signal, d_key, "tn"))
    window_sum.put(2, dot(signal, d_value, "tn"))
    window_sum.to_core()
    signal_grad = (
        own_grads.astype(F32)
        + dot(d_query, wq[...], "nt")
        + dot(d_key, wk[...], "nt")
        + dot(d_value, wv[...], "nt")
    )
    sg_out[...] = signal_grad.astype(BF16).reshape(2, 256, 256)
    window_sum.to_plane()
    station_sum.to_line()
    window_sum.to_line()
    station_sum.back()
    window_sum.back()
    station_sum.pass_on()
    for copy in to_output:
        copy.wait_recv()
    bo_out[...] = bo[...]
    window_sum.pass_on()
    station_sum.finish()
    for copy in [*halos, *to_frames, *to_rows, *rims, *to_owner, *to_rims, *to_output]:
        copy.wait_send()
    fin_out[1536:4096, :] = station_sum.fin[...]
    window_sum.finish()
    fin_out[0:1536, :] = window_sum.fin[...]


def sum_scratch(count):
    dma = pltpu.SemaphoreType.DMA
    rows = count * 16
    return [
        pltpu.VMEM((count * 512, LANES), BF16),
        pltpu.VMEM((count * 256, LANES), BF16),
        pltpu.VMEM((count * 256, LANES), BF16),
        pltpu.VMEM((15, rows, LANES), BF16),
        pltpu.VMEM((8, rows, LANES), BF16),
        pltpu.VMEM((count * 512, LANES), BF16),
        dma((2,)), dma((15,)), dma((15,)), dma((7,)), dma((7,)),
        dma((15,)), dma((15,)), dma((16,)), dma((16,)),
    ]


def finish_kernel(factor, bo, sg, fin, o_bo, o_sg, *rest):
    outs, (wide, sem) = rest[:8], rest[8:]
    copies = [
        pltpu.make_async_copy(bo, o_bo, sem.at[8]),
        pltpu.make_async_copy(sg, o_sg, sem.at[9]),
    ]
    for copy in copies:
        copy.start()
    for i, ref in enumerate(outs):
        for j in range(2):
            wide[i, :, j * LANES : (j + 1) * LANES] = (
                fin[pl.ds((2 * i + j) * 256, 256), :].astype(F32) * factor
            )
        copies.append(pltpu.make_async_copy(wide.at[i], ref, sem.at[i]))
        copies[-1].start()
    for copy in copies:
        copy.wait()


def body(signal, cotangent, *rest):
    dma = pltpu.SemaphoreType.DMA
    vmem = pl.BlockSpec(memory_space=pltpu.VMEM)
    hbm = pl.BlockSpec(memory_space=pltpu.HBM)

    def b(*shape):
        return pltpu.VMEM(shape, BF16)

    def f(*shape):
        return pltpu.VMEM(shape, F32)

    words = pltpu.VMEM((16, 32), jnp.int32)
    scratch = [
        b(2, 256, 256), b(8, 256, 256), words, words,
        b(2, 512, 256), b(2, 512, 256), b(2, 512, 256), b(2, 512, 256), b(2, 512, 256),
        f(4, 2, 1, 512), f(2, 256, 512), f(2, 128, 512), f(2, 128, 512), f(4, 1, 512), f(4, 1, 512),
        f(4, 256, 512), f(4, 128, 512), f(4, 128, 512), b(2, 256, 256),
        b(32, 16, 256), b(32, 16, 256), f(128, 512), f(128, 512), b(512, 512), b(512, 512),
        b(512, 256), b(512, 256), b(512, 256), b(512, 256),
        b(512, 256), b(512, 256), b(512, 256), b(512, 256),
        b(32, 16, 256), b(32, 16, 256), b(2, 256, 256),
        b(2, 512, 256), b(2, 512, 256), f(4, 2, 1, 512), b(2, 256, 256),
        dma((12,)), dma((6,)), dma((6,)), dma((5, 15)), dma((5, 15)), dma((16,)), dma((16,)),
        *sum_scratch(5), *sum_scratch(3),
    ]
    *inputs, neighbours, neighbour_valid = (signal, cotangent, *rest)
    block_output, signal_grad, fin = pl.pallas_call(
        block_kernel,
        out_shape=[
            jax.ShapeDtypeStruct((2, 256, 256), BF16),
            jax.ShapeDtypeStruct((2, 256, 256), BF16),
            jax.ShapeDtypeStruct((4096, LANES), BF16),
        ],
        in_specs=[hbm] * 12,
        out_specs=[vmem] * 3,
        scratch_shapes=scratch,
        compiler_params=pltpu.CompilerParams(
            collective_id=0, has_side_effects=True, vmem_limit_bytes=48 * 1024 * 1024
        ),
        name="block",
    )(*inputs, neighbours.T, neighbour_valid.T)
    factor = 1.0 / math.sqrt(STN * 2 * TM * 256)
    order = pl.pallas_call(
        functools.partial(finish_kernel, factor),
        out_shape=[
            jax.ShapeDtypeStruct((2, 256, 256), BF16),
            jax.ShapeDtypeStruct((2, 256, 256), BF16),
        ]
        + [jax.ShapeDtypeStruct((256, 256), F32)] * 8,
        in_specs=[vmem] * 3,
        out_specs=[hbm] * 10,
        scratch_shapes=[f(8, 256, 256), dma((10,))],
        compiler_params=pltpu.CompilerParams(vmem_limit_bytes=8 * 1024 * 1024),
        name="finish",
    )(block_output, signal_grad, fin)
    bo, sg, wq, wk, wv, sq, sk, sv, so, wo = order
    return bo, sg, wq, wk, wv, wo, sq, sk, sv, so


def solution(mesh):
    return jax.shard_map(
        lambda *operands: tuple(body(*operands)),
        mesh=mesh,
        in_specs=(P("stn", "tm", None), P("stn", "tm", None), *([P()] * 10)),
        out_specs=(P("stn", "tm", None), P("stn", "tm", None), *([P()] * 8)),
        check_vma=False,
    )
```

time: 102 us -> 87 us (0.85)
  Pallas kernels: 88.1 us -> 75.3 us
  local copies, waits for them, and re-layouts: 12.4 us -> 10.5 us
    pallas_call x1, Pallas kernels: 85.2 us -> 73.7 us  [body(): pl.pallas_call(block_kernel, out_shape=[jax.ShapeDtypeStruct((2, 256, 256...]
    unnamed x30 -> x24, local copies, waits for them, and re-layouts: 12.4 us -> 10.5 us
    pallas_call x1, Pallas kernels: 2.89 us -> 1.57 us  [body(): pl.pallas_call(functools.partial(finish_kernel, factor), out_shape=[jax.S...]
where the time goes in v3:
time: 87 us; the launch traced here: 86.7 us
  Pallas kernels  75.3 us (87%)
  local copies, waits for them, and re-layouts  10.5 us (12%)
    pallas_call x1, Pallas kernels, body(): pl.pallas_call(block_kernel, out_shape=[jax.ShapeDtypeStruct((2, 256, 256...  73.7 us
    unnamed x24, local copies, waits for them, and re-layouts  10.5 us

profile of v3, /device:TPU:1, one launch (start us, length us, event | category | flops | bytes accessed | tf_op | source)
XLA Modules:
  0.0 86.7 jit_solution(14335563969778911078)
XLA Ops:
  0.6 0.0 copy-start
  0.7 0.9 %copy-done = bf16[2,256,256]{2,1,0:T(8,128)(2,1)S(1)} copy-done((bf16[2,256,256]{2,1,0:T(8,128)(2,1)S(1)}, bf16[2,256,256]{2,1,0:T(8,128)(2,1)}, u32[]{:S(2)}) %copy-start) | copy-done | bytes 262168
  1.6 0.0 copy-start.1
  1.6 0.9 %copy-done.1 = bf16[2,256,256]{2,1,0:T(8,128)(2,1)S(1)} copy-done((bf16[2,256,256]{2,1,0:T(8,128)(2,1)S(1)}, bf16[2,256,256]{2,1,0:T(8,128)(2,1)}, u32[]{:S(2)}) %copy-start.1) | copy-done | bytes 262168
  2.5 0.0 copy-start.2
  2.6 0.9 %copy-done.2 = bf16[256,256]{1,0:T(8,128)(2,1)S(1)} copy-done((bf16[256,256]{1,0:T(8,128)(2,1)S(1)}, bf16[256,256]{1,0:T(8,128)(2,1)}, u32[]{:S(2)}) %copy-start.2) | copy-done | bytes 131096
  3.5 0.0 copy-start.3
  3.5 0.9 %copy-done.3 = bf16[256,256]{1,0:T(8,128)(2,1)S(1)} copy-done((bf16[256,256]{1,0:T(8,128)(2,1)S(1)}, bf16[256,256]{1,0:T(8,128)(2,1)}, u32[]{:S(2)}) %copy-start.3) | copy-done | bytes 131096
  4.4 0.0 copy-start.4
  4.4 0.9 %copy-done.4 = bf16[256,256]{1,0:T(8,128)(2,1)S(1)} copy-done((bf16[256,256]{1,0:T(8,128)(2,1)S(1)}, bf16[256,256]{1,0:T(8,128)(2,1)}, u32[]{:S(2)}) %copy-start.4) | copy-done | bytes 131096
  5.3 0.0 copy-start.5
  5.3 0.9 %copy-done.5 = bf16[256,256]{1,0:T(8,128)(2,1)S(1)} copy-done((bf16[256,256]{1,0:T(8,128)(2,1)S(1)}, bf16[256,256]{1,0:T(8,128)(2,1)}, u32[]{:S(2)}) %copy-start.5) | copy-done | bytes 131096
  6.2 0.0 copy-start.6
  6.2 0.9 %copy-done.6 = bf16[256,256]{1,0:T(8,128)(2,1)S(1)} copy-done((bf16[256,256]{1,0:T(8,128)(2,1)S(1)}, bf16[256,256]{1,0:T(8,128)(2,1)}, u32[]{:S(2)}) %copy-start.6) | copy-done | bytes 131096
  7.1 0.0 copy-start.7
  7.1 0.9 %copy-done.7 = bf16[256,256]{1,0:T(8,128)(2,1)S(1)} copy-done((bf16[256,256]{1,0:T(8,128)(2,1)S(1)}, bf16[256,256]{1,0:T(8,128)(2,1)}, u32[]{:S(2)}) %copy-start.7) | copy-done | bytes 131096
  8.0 0.0 copy-start.8
  8.0 0.9 %copy-done.8 = bf16[256,256]{1,0:T(8,128)(2,1)S(1)} copy-done((bf16[256,256]{1,0:T(8,128)(2,1)S(1)}, bf16[256,256]{1,0:T(8,128)(2,1)}, u32[]{:S(2)}) %copy-start.8) | copy-done | bytes 131096
  8.9 0.0 copy-start.9
  8.9 0.9 %copy-done.9 = bf16[256,256]{1,0:T(8,128)(2,1)S(1)} copy-done((bf16[256,256]{1,0:T(8,128)(2,1)S(1)}, bf16[256,256]{1,0:T(8,128)(2,1)}, u32[]{:S(2)}) %copy-start.9) | copy-done | bytes 131096
  9.8 0.0 copy-start.10
  9.8 0.7 copy-done.10
  10.5 0.0 copy-start.11
  10.5 0.7 copy-done.11
  11.2 73.7 %block.1 = (bf16[2,256,256]{2,1,0:T(8,128)(2,1)S(1)}, bf16[2,256,256]{2,1,0:T(8,128)(2,1)S(1)}, bf16[4096,128]{1,0:T(8,128)(2,1)S(1)}) custom-call(bf16[2,256,256]{2,1,0:T(8,128)(2,1)S(1)} %copy-done, bf16[2,256,256]{2,1,0:T(8,128)(2,1)S(1)} %copy-done.1, bf16[256,256]{1,0:T(8,128)(2,1)S(1)} %copy-done.2, bf16[256,256]{1,0:T(8,128)(2,1)S(1)} %copy-done.3, ...), custom_call_target="tpu_custom_call" | custom-call | tf_op jit(solution)/shard_map/block/pallas_call | solution.py:591
  84.9 1.6 %finish.1 = (bf16[2,256,256]{2,1,0:T(8,128)(2,1)}, bf16[2,256,256]{2,1,0:T(8,128)(2,1)}, f32[256,256]{1,0:T(8,128)}, f32[256,256]{1,0:T(8,128)}, f32[256,256]{1,...) custom-call(bf16[2,256,256]{2,1,0:T(8,128)(2,1)S(1)} %get-tuple-elem, ...), custom_call_target="tpu_custom_call" | custom-call | tf_op jit(solution)/shard_map/finish/pallas_call | solution.py:607
Async XLA Ops:
  0.6 1.0 %copy-start = (bf16[2,256,256]{2,1,0:T(8,128)(2,1)S(1)}, bf16[2,256,256]{2,1,0:T(8,128)(2,1)}, u32[]{:S(2)}) copy-start(bf16[2,256,256]{2,1,0:T(8,128)(2,1)} %sig_in.1) | copy-start | bytes 786436
  1.6 0.9 %copy-start.1 = (bf16[2,256,256]{2,1,0:T(8,128)(2,1)S(1)}, bf16[2,256,256]{2,1,0:T(8,128)(2,1)}, u32[]{:S(2)}) copy-start(bf16[2,256,256]{2,1,0:T(8,128)(2,1)} %cot.1) | copy-start | bytes 786436
  2.5 0.9 %copy-start.2 = (bf16[256,256]{1,0:T(8,128)(2,1)S(1)}, bf16[256,256]{1,0:T(8,128)(2,1)}, u32[]{:S(2)}) copy-start(bf16[256,256]{1,0:T(8,128)(2,1)} %wq_in.1) | copy-start | bytes 393220
  3.5 0.9 %copy-start.3 = (bf16[256,256]{1,0:T(8,128)(2,1)S(1)}, bf16[256,256]{1,0:T(8,128)(2,1)}, u32[]{:S(2)}) copy-start(bf16[256,256]{1,0:T(8,128)(2,1)} %wk_in.1) | copy-start | bytes 393220
  4.4 0.9 %copy-start.4 = (bf16[256,256]{1,0:T(8,128)(2,1)S(1)}, bf16[256,256]{1,0:T(8,128)(2,1)}, u32[]{:S(2)}) copy-start(bf16[256,256]{1,0:T(8,128)(2,1)} %wv_in.1) | copy-start | bytes 393220
  5.3 0.9 %copy-start.5 = (bf16[256,256]{1,0:T(8,128)(2,1)S(1)}, bf16[256,256]{1,0:T(8,128)(2,1)}, u32[]{:S(2)}) copy-start(bf16[256,256]{1,0:T(8,128)(2,1)} %wo_in.1) | copy-start | bytes 393220
  6.2 0.9 %copy-start.6 = (bf16[256,256]{1,0:T(8,128)(2,1)S(1)}, bf16[256,256]{1,0:T(8,128)(2,1)}, u32[]{:S(2)}) copy-start(bf16[256,256]{1,0:T(8,128)(2,1)} %sq_in.1) | copy-start | bytes 393220
  7.1 0.9 %copy-start.7 = (bf16[256,256]{1,0:T(8,128)(2,1)S(1)}, bf16[256,256]{1,0:T(8,128)(2,1)}, u32[]{:S(2)}) copy-start(bf16[256,256]{1,0:T(8,128)(2,1)} %sk_in.1) | copy-start | bytes 393220
  8.0 0.9 %copy-start.8 = (bf16[256,256]{1,0:T(8,128)(2,1)S(1)}, bf16[256,256]{1,0:T(8,128)(2,1)}, u32[]{:S(2)}) copy-start(bf16[256,256]{1,0:T(8,128)(2,1)} %sv_in.1) | copy-start | bytes 393220
  8.9 0.9 %copy-start.9 = (bf16[256,256]{1,0:T(8,128)(2,1)S(1)}, bf16[256,256]{1,0:T(8,128)(2,1)}, u32[]{:S(2)}) copy-start(bf16[256,256]{1,0:T(8,128)(2,1)} %so_in.1) | copy-start | bytes 393220
  9.8 0.7 copy-start.10
  10.5 0.7 copy-start.11
